TPU v7x, 32 devices: a whole 2x2x4 slice. The times are simulated.
32 devices in a mesh: batch: 4 (over z), seq: 2 (over core), ch: 4 (over y, x).
Axes of the slice: x: 2, y: 2, z: 4, core: 2. Of those that a mesh axis runs over, the one named last changes fastest.
Arguments:
- inputs: bfloat16 [16, 1280, 2048], P('batch', 'ch', 'seq'), may hold values from -6 to 6
- segment_ids: int32 [16, 2048], P('batch', 'seq'), may hold values from 0 to 7, never falling along the last dimension, each value on 1 to 512 neighbouring positions
- norm0_gain: float32 [1280], P('ch'), may hold values from 0.1 to 1.9
- norm0_shift: float32 [1280], P('ch'), may hold values from -3 to 3
- w_inner: bfloat16 [1280, 640], P('ch'), may hold values from -0.15625 to 0.15625
- b_inner: float32 [640], P('ch'), may hold values from -3 to 3
- norm1_gain: float32 [640], P('ch'), may hold values from 0.1 to 1.9
- norm1_shift: float32 [640], P('ch'), may hold values from -3 to 3
- w_conv: bfloat16 [5, 640, 640], P(None, 'ch'), may hold values from -0.109375 to 0.109375
- b_conv: float32 [640], P('ch'), may hold values from -3 to 3
- norm2_gain: float32 [640], P('ch'), may hold values from 0.1 to 1.9
- norm2_shift: float32 [640], P('ch'), may hold values from -3 to 3
- w_outer: bfloat16 [640, 1280], P('ch'), may hold values from -0.25 to 0.25
- b_outer: float32 [1280], P('ch'), may hold values from -3 to 3
- cotangent: bfloat16 [16, 1280, 2048], P('batch', 'ch', 'seq'), may hold values from -6 to 6
Outputs:
- output: bfloat16 [16, 1280, 2048], P('batch', 'ch', 'seq')
- input_grad: bfloat16 [16, 1280, 2048], P('batch', 'ch', 'seq')
- grad_norm0_gain: float32 [1280], P('ch')
- grad_norm0_shift: float32 [1280], P('ch')
- grad_w_inner: float32 [1280, 640], P('ch')
- grad_b_inner: float32 [640], P('ch')
- grad_norm1_gain: float32 [640], P('ch')
- grad_norm1_shift: float32 [640], P('ch')
- grad_w_conv: float32 [5, 640, 640], P(None, 'ch')
- grad_b_conv: float32 [640], P('ch')
- grad_norm2_gain: float32 [640], P('ch')
- grad_norm2_shift: float32 [640], P('ch')
- grad_w_outer: float32 [640, 1280], P('ch')
- grad_b_outer: float32 [1280], P('ch')
Inputs may be any that keep to these rules, and one draw needn't show every extreme that they name: `segment_ids`: along a row the ids never fall; each protein is one run of 1 to 512 residues, one run of each row has exactly 512, and every row holds all 8 ids.
All inputs are finite; a program needn't handle non-finite values.
Results may differ from a plain program's by a relative error of at most 0.0065.
Values may be sent and summed in bfloat16 or wider, within the bound.
A program may use at most 192 MiB of HBM per device.

v0:
```python
import functools
import math

import jax
import jax.numpy as jnp
from jax import lax
from jax.experimental import pallas as pl
from jax.experimental.pallas import tpu as pltpu
from jax.sharding import PartitionSpec as P

KERNEL_TAPS = 5
DILATION_SPACING = 32


EPSILON = 1e-05


MESH_AXES = ("batch", "seq", "ch")
MESH_ID = pl.DeviceIdType.MESH


def _group_index(group, sizes, coords):
    me = 0
    for a in group:
        me = me * sizes[a] + coords[a]
    return me


def _exchange_kernel(sizes, group, gather, reduce, axes, *refs):
    count_arrays = len(axes)
    x_refs = refs[:count_arrays]
    o_refs = refs[count_arrays : 2 * count_arrays]
    send_sem, recv_sem = refs[2 * count_arrays :]
    coords = {a: lax.axis_index(a) for a in MESH_AXES}
    me = _group_index(group, sizes, coords)
    count = math.prod(sizes[a] for a in group)

    def device(index):
        where = dict(coords)
        rest = index
        for a in reversed(group):
            where[a] = lax.rem(rest, sizes[a])
            rest = rest // sizes[a]
        return tuple(where[a] for a in MESH_AXES)

    barrier = pltpu.get_barrier_semaphore()
    for j in range(1, count):
        pl.semaphore_signal(barrier, 1, device_id=device(lax.rem(me + j, count)), device_id_type=MESH_ID)
    pl.semaphore_wait(barrier, count - 1)
    copies = []
    for j in range(1, count):
        peer = lax.rem(me + j, count)
        for i in range(count_arrays):
            lead = (slice(None),) * axes[i]
            if gather:
                src, dst = x_refs[i], o_refs[i].at[me]
            else:
                slot = (j - 1) if reduce else me
                src = x_refs[i].at[lead + (pl.ds(peer, 1),)]
                dst = o_refs[i].at[lead + (pl.ds(slot, 1),)]
            copy = pltpu.make_async_remote_copy(
                src_ref=src,
                dst_ref=dst,
                send_sem=send_sem.at[i, j - 1],
                recv_sem=recv_sem.at[i, j - 1],
                device_id=device(peer),
                device_id_type=MESH_ID,
            )
            copy.start()
            copies.append(copy)
    for copy in copies:
        copy.wait()


def exchange(xs, group, collective_id, gather=False, axes=None, reduce=False):
    sizes = {a: lax.axis_size(a) for a in MESH_AXES}
    count = math.prod(sizes[a] for a in group)
    axes = tuple(axes or (0,) * len(xs))
    if count == 1:
        return [x[None] if gather else x for x in xs]
    shapes = [jax.ShapeDtypeStruct((count,) + x.shape if gather else x.shape, x.dtype) for x in xs]
    if reduce:
        shapes = [
            jax.ShapeDtypeStruct(x.shape[:a] + (count - 1,) + x.shape[a + 1 :], x.dtype) for x, a in zip(xs, axes)
        ]
    moved = sum(x.size * x.dtype.itemsize * (count if gather else 1) for x in xs)
    outs = pl.pallas_call(
        functools.partial(_exchange_kernel, sizes, group, gather, reduce, axes),
        out_shape=shapes,
        in_specs=[pl.BlockSpec(memory_space=pl.ANY)] * len(xs),
        out_specs=[pl.BlockSpec(memory_space=pl.ANY)] * len(xs),
        scratch_shapes=[
            pltpu.SemaphoreType.DMA((len(xs), count - 1)),
            pltpu.SemaphoreType.DMA((len(xs), count - 1)),
        ],
        compiler_params=pltpu.CompilerParams(collective_id=collective_id, has_side_effects=True),
        cost_estimate=pl.CostEstimate(flops=0, transcendentals=0, bytes_accessed=2 * moved),
    )(*xs)
    me = _group_index(group, sizes, {a: lax.axis_index(a) for a in group})
    placed = []
    if reduce:
        for x, out, axis in zip(xs, outs, axes):
            own = lax.dynamic_index_in_dim(x, me, axis, keepdims=False)
            placed.append(own + jnp.sum(out, axis=axis))
        return placed
    for x, out, axis in zip(xs, outs, axes):
        own = x if gather else lax.dynamic_index_in_dim(x, me, axis, keepdims=False)
        placed.append(lax.dynamic_update_index_in_dim(out, own, me, axis))
    return placed


def gelu_exact(values):
    return jax.nn.gelu(values, approximate=False)


def gelu_back(point, grad):
    return jax.vjp(gelu_exact, point)[1](grad)[0]


def normalize(values, gain, shift):
    center = jnp.mean(values, axis=1, keepdims=True)
    offset = values - center
    spread = jnp.mean(offset * offset, axis=1, keepdims=True)
    scale = lax.rsqrt(spread + EPSILON)
    unit = offset * scale
    return (unit * gain[:, None] + shift[:, None], unit, scale)


def normalize_back(grad, unit, scale, gain):
    scaled = grad * gain[:, None]
    first = jnp.mean(scaled, axis=1, keepdims=True)
    second = jnp.mean(scaled * unit, axis=1, keepdims=True)
    return scale * (scaled - first - unit * second)


def neighbour_pairs(seqs, nch, q_count):
    pairs = []
    for s in range(seqs):
        for c in range(nch):
            q = c % q_count
            if q < q_count - 1:
                pairs.append((s * nch + c, s * nch + c + 1))
            elif s < seqs - 1:
                pairs.append((s * nch + c, (s + 1) * nch + c - (q_count - 1)))
    return pairs


def extended(x, width, pairs):
    down = [(j, i) for i, j in pairs]
    length = x.shape[-1]
    before = lax.ppermute(x[..., length - width :], ("seq", "ch"), pairs)
    after = lax.ppermute(x[..., :width], ("seq", "ch"), down)
    return jnp.concatenate([before, x, after], axis=-1)


def shifted_taps(wide, wide_ids, own_ids, offsets, border):
    length = own_ids.shape[-1]
    pieces = []
    for offset in offsets:
        lower = border + offset
        shifted = wide[:, :, lower : lower + length]
        matching = wide_ids[:, lower : lower + length] == own_ids
        pieces.append(jnp.where(matching[:, None, :], shifted, jnp.zeros_like(shifted)))
    return jnp.concatenate(pieces, axis=1)


def to_positions(x, nch, q_count):
    rows, width, length = x.shape
    if q_count > 1:
        x = x.reshape(rows, width, q_count, length // q_count).transpose(0, 2, 1, 3)
        x = x.reshape(rows * q_count, width, length // q_count)
    x = lax.all_to_all(x, "ch", 0, 0, tiled=True)
    return _join(x, nch)


def _join(x, nch):
    total, width, length = x.shape
    p = total // nch
    return x.reshape(nch, p, width, length).transpose(1, 0, 2, 3).reshape(p, nch * width, length)


def to_channels(x, nch, q_count, rows):
    p, width, length = x.shape
    x = x.reshape(p, nch, width // nch, length).transpose(1, 0, 2, 3).reshape(nch * p, width // nch, length)
    x = lax.all_to_all(x, "ch", 0, 0, tiled=True)
    if q_count > 1:
        _, width, part = x.shape
        x = x.reshape(rows, q_count, width, part).transpose(0, 2, 1, 3).reshape(rows, width, q_count * part)
    return x


def local(
    inputs,
    segment_ids,
    norm0_gain,
    norm0_shift,
    w_inner,
    b_inner,
    norm1_gain,
    norm1_shift,
    w_conv,
    b_conv,
    norm2_gain,
    norm2_shift,
    w_outer,
    b_outer,
    cotangent,
):
    nch = lax.axis_size("ch")
    seqs = lax.axis_size("seq")
    batches = lax.axis_size("batch")
    rows, dloc, length = inputs.shape
    hloc = w_conv.shape[1]
    hid = hloc * nch
    dim = dloc * nch
    if rows % nch == 0:
        q_count = 1
    else:
        q_count = nch // rows
    part = length // q_count
    border = 2 * DILATION_SPACING
    offsets = [(k - KERNEL_TAPS // 2) * DILATION_SPACING for k in range(KERNEL_TAPS)]
    back_offsets = [-o for o in offsets]
    pairs = neighbour_pairs(seqs, nch, q_count)
    me = lax.axis_index("ch")

    smalls = [norm0_gain, norm0_shift, b_inner, norm1_gain, norm1_shift, b_conv, norm2_gain, norm2_shift, b_outer]
    sidx = lax.axis_index("seq")
    halves = [
        lax.dynamic_slice_in_dim(w_inner, sidx * (dloc // seqs), dloc // seqs, 0),
        lax.dynamic_slice_in_dim(w_conv, sidx * (hloc // seqs), hloc // seqs, 1),
        lax.dynamic_slice_in_dim(w_outer, sidx * (hloc // seqs), hloc // seqs, 0),
    ]
    small_all, w_in, w_out = exchange([jnp.concatenate(smalls), halves[0], halves[2]], ("ch",), 0, gather=True)
    w_cv = lax.all_gather(halves[1], "ch", axis=0)
    cut = 0
    full = []
    for v in smalls:
        n = v.shape[0]
        full.append(small_all[:, cut : cut + n].reshape(n * nch))
        cut += n
    g0, s0, b_in, g1, s1, b_cv, g2, s2, b_out = full
    w_in = lax.all_gather(w_in, "seq", axis=1, tiled=True).reshape(dim, hid)
    w_cv = lax.all_gather(w_cv, "seq", axis=2, tiled=True).transpose(1, 0, 2, 3).reshape(KERNEL_TAPS, hid, hid)
    w_out = lax.all_gather(w_out, "seq", axis=1, tiled=True).reshape(hid, dim)

    x = to_positions(inputs, nch, q_count)
    cot = to_positions(cotangent, nch, q_count)
    prow = x.shape[0]
    if q_count == 1:
        ids = lax.dynamic_slice_in_dim(segment_ids, me * prow, prow, axis=0)
    else:
        ids = lax.dynamic_slice_in_dim(segment_ids, me // q_count, 1, axis=0)
        ids = lax.dynamic_slice_in_dim(ids, (me % q_count) * part, part, axis=1)
    own_ids = ids + 1
    wide_ids = extended(own_ids, border, pairs)

    residual = x.astype(jnp.float32)
    normed0, unit0, scale0 = normalize(residual, g0, s0)
    hidden0 = gelu_exact(normed0).astype(jnp.bfloat16)
    inner = jnp.einsum("dh,rdl->rhl", w_in, hidden0, preferred_element_type=jnp.float32) + b_in[:, None]
    normed1, unit1, scale1 = normalize(inner, g1, s1)
    hidden1 = gelu_exact(normed1).astype(jnp.bfloat16)
    wide_hidden = extended(hidden1, border, pairs)
    taps = shifted_taps(wide_hidden, wide_ids, own_ids, offsets, border)
    kernel_flat = w_cv.reshape(KERNEL_TAPS * hid, hid)
    mixed = jnp.einsum("co,rcl->rol", kernel_flat, taps, preferred_element_type=jnp.float32) + b_cv[:, None]
    normed2, unit2, scale2 = normalize(mixed, g2, s2)
    hidden2 = gelu_exact(normed2).astype(jnp.bfloat16)
    branch = jnp.einsum("hd,rhl->rdl", w_out, hidden2, preferred_element_type=jnp.float32)
    output = (residual + branch + b_out[:, None]).astype(jnp.bfloat16)
    output = to_channels(output, nch, q_count, rows)

    grad_b_outer = jnp.sum(cot.astype(jnp.float32), axis=(0, 2))
    grad_w_outer = jnp.einsum("rhl,rdl->hd", hidden2, cot, preferred_element_type=jnp.float32)
    def reduce_seq_batch(g, split_dim, after=None):
        if after is not None:
            g, _ = lax.optimization_barrier((g, after))
        g = lax.psum_scatter(g, "seq", scatter_dimension=split_dim, tiled=True)
        return lax.psum_scatter(g, "batch", scatter_dimension=split_dim, tiled=True)

    part_outer = reduce_seq_batch(grad_w_outer.reshape(nch, hloc * dim // 128, 128), 1)
    grad_hidden2 = jnp.einsum("hd,rdl->rhl", w_out, cot, preferred_element_type=jnp.float32)
    grad_normed2 = gelu_back(normed2, grad_hidden2)
    grad_norm2_gain = jnp.sum(grad_normed2 * unit2, axis=(0, 2))
    grad_norm2_shift = jnp.sum(grad_normed2, axis=(0, 2))
    grad_mixed = normalize_back(grad_normed2, unit2, scale2, g2).astype(jnp.bfloat16)
    grad_b_conv = jnp.sum(grad_mixed.astype(jnp.float32), axis=(0, 2))
    grad_w_conv = jnp.einsum(
        "rol,rkcil->okci",
        grad_mixed,
        taps.reshape(prow, KERNEL_TAPS, nch, hloc, part),
        preferred_element_type=jnp.float32,
    )
    wide_grad = extended(grad_mixed, border, pairs)
    back_taps = shifted_taps(wide_grad, wide_ids, own_ids, back_offsets, border)
    kernel_back = jnp.transpose(w_cv, (0, 2, 1)).reshape(KERNEL_TAPS * hid, hid)
    grad_hidden1 = jnp.einsum("oc,rol->rcl", kernel_back, back_taps, preferred_element_type=jnp.float32)
    grad_normed1 = gelu_back(normed1, grad_hidden1)
    grad_norm1_gain = jnp.sum(grad_normed1 * unit1, axis=(0, 2))
    grad_norm1_shift = jnp.sum(grad_normed1, axis=(0, 2))
    grad_inner = normalize_back(grad_normed1, unit1, scale1, g1).astype(jnp.bfloat16)
    grad_inner, _, output = lax.optimization_barrier((grad_inner, part_outer, output))
    grad_b_inner = jnp.sum(grad_inner.astype(jnp.float32), axis=(0, 2))
    grad_w_inner = jnp.einsum("rdl,rhl->dh", hidden0, grad_inner, preferred_element_type=jnp.float32)
    grad_hidden0 = jnp.einsum("dh,rhl->rdl", w_in, grad_inner, preferred_element_type=jnp.float32)
    grad_normed0 = gelu_back(normed0, grad_hidden0)
    grad_norm0_gain = jnp.sum(grad_normed0 * unit0, axis=(0, 2))
    grad_norm0_shift = jnp.sum(grad_normed0, axis=(0, 2))
    input_grad = (cot.astype(jnp.float32) + normalize_back(grad_normed0, unit0, scale0, g0)).astype(jnp.bfloat16)


    vectors = [
        grad_norm0_gain,
        grad_norm0_shift,
        grad_b_inner,
        grad_norm1_gain,
        grad_norm1_shift,
        grad_b_conv,
        grad_norm2_gain,
        grad_norm2_shift,
        grad_b_outer,
    ]
    flat = jnp.concatenate([v.reshape(nch, -1) for v in vectors], axis=1)
    vec_len = flat.shape[1]
    inner_rows = dloc * hid // 128
    stack_rows = -(-(inner_rows + -(-vec_len // 128)) // (seqs * batches * 8)) * (seqs * batches * 8)
    vec_rows = stack_rows - inner_rows
    flat = jnp.pad(flat, ((0, 0), (0, vec_rows * 128 - vec_len))).reshape(nch, vec_rows, 128)
    inner_plus = jnp.concatenate([grad_w_inner.reshape(nch, inner_rows, 128), flat], axis=1)

    conv_tail = grad_w_conv.shape[1:]
    def finish(part, axis, cid):
        part = exchange([part], ("ch",), cid, axes=(axis,), reduce=True)[0]
        shape = part.shape
        if part.size % 128 == 0:
            part = part.reshape(part.size // 128, 128)
        part = lax.all_gather(part, "batch", axis=0)
        return lax.all_gather(part, "seq", axis=0, tiled=True).reshape((seqs * batches,) + shape)

    part_conv = reduce_seq_batch(grad_w_conv.reshape(hid, math.prod(conv_tail) // 128, 128), 0, part_outer)
    part_conv = part_conv.reshape((part_conv.shape[0],) + conv_tail)
    red_outer = finish(part_outer, 0, 1)
    inner_plus, red_outer = lax.optimization_barrier((inner_plus, red_outer))
    part_inner = reduce_seq_batch(inner_plus, 1, part_conv)
    red_conv = finish(part_conv, 2, 2)
    input_grad, red_conv = lax.optimization_barrier((input_grad, red_conv))
    input_grad = to_channels(input_grad, nch, q_count, rows)
    red_inner = finish(part_inner, 0, 3)
    red_w_outer = red_outer.reshape(hloc, dim)
    red_w_conv = red_conv.reshape(hid, KERNEL_TAPS, hloc).transpose(1, 2, 0)
    red_inner = red_inner.reshape(-1)
    red_w_inner = red_inner[: dloc * hid].reshape(dloc, hid)
    mine = red_inner[dloc * hid : dloc * hid + vec_len]
    reds = []
    cut = 0
    for v in vectors:
        n = v.shape[0] // nch
        reds.append(mine[cut : cut + n])
        cut += n
    return (
        output,
        input_grad,
        reds[0],
        reds[1],
        red_w_inner,
        reds[2],
        reds[3],
        reds[4],
        red_w_conv,
        reds[5],
        reds[6],
        reds[7],
        red_w_outer,
        reds[8],
    )


def solution(mesh):
    return jax.shard_map(
        local,
        mesh=mesh,
        in_specs=(
            P("batch", "ch", "seq"),
            P("batch", "seq"),
            P("ch"),
            P("ch"),
            P("ch", None),
            P("ch"),
            P("ch"),
            P("ch"),
            P(None, "ch", None),
            P("ch"),
            P("ch"),
            P("ch"),
            P("ch", None),
            P("ch"),
            P("batch", "ch", "seq"),
        ),
        out_specs=(
            P("batch", "ch", "seq"),
            P("batch", "ch", "seq"),
            P("ch"),
            P("ch"),
            P("ch", None),
            P("ch"),
            P("ch"),
            P("ch"),
            P(None, "ch", None),
            P("ch"),
            P("ch"),
            P("ch"),
            P("ch", None),
            P("ch"),
        ),
        check_vma=False,
    )
```

profile of v0, /device:TPU:0, one launch (start us, length us, event | category | flops | bytes accessed | tf_op | source)
XLA Modules:
  0.0 530.7 jit_solution(1401888643741242362)
XLA Ops:
  12.1 23.3 %shard_map.254 = (f32[4,1920]{1,0:T(4,128)}, bf16[4,160,640]{2,1,0:T(8,128)(2,1)}, bf16[4,80,1280]{2,1,0:T(8,128)(2,1)}) custom-call(f32[1920]{0:T(1024)} %concatenate.42.refs_0_, bf16[160,640]{1,0:T(8,128)(2,1)} %constant_dynamic-slice_fusion.2.refs_1_, bf16[80,1280]{1,0:T(8,128)(2,1)} %constant_dynamic-slice_fusion.1.refs_2_), custom_call_target="tpu_custom_call" | custom-call | bytes 3338240 | tf_op jit(solution)/shard_map/pallas_call | solution.py:87
  37.0 4.7 all-to-all-start
  43.9 3.0 collective-permute-start.1
  48.7 29.4 %all-to-all-done = bf16[4,320,1024]{2,1,0:T(8,128)(2,1)} async-done(((bf16[4,320,1024]{2,1,0:T(8,128)(2,1)}), bf16[4,320,1024]{2,1,0:T(8,128)(2,1)}, u32[]{:S(2)}, u32[]{:S(2)}) %all-to-all-start) | async-done | bytes 2621472 | tf_op jit(solution)/shard_map/all_to_all | solution.py:172
  78.1 4.6 all-to-all-start.1
  92.4 14.3 %fusion.6 = bf16[1,1280,1,1,1,1,1024]{6,1,5,4,3,2,0:T(8,128)(2,1)} fusion(f32[1,1280,1,1,1,1,1024]{6,1,5,4,3,2,0:T(8,128)S(1)} %bitcast.258, f32[1280]{0:T(1024)S(1)} %add.196, f32[1280]{0:T(1024)S(1)} %mul.439, f32[1024]{0:T(1024)S(1)} %add_rsqrt_fusion.2, f32[1024]{0:T(1024)S(1)} %broadcast_multiply_fusion.8), kind=kLoop, calls=%fused_computation.8 | loop fusion | flops 90439680 | bytes 7882752 | tf_op jit(solution)/shard_map/convert_element_type | solution.py:260
  106.7 4.6 fusion.72
  113.4 8.6 %all-gather.15.cloned.1.call-done = bf16[20,80,640]{2,1,0:T(8,128)(2,1)} async-done(((bf16[5,80,640]{2,1,0:T(8,128)(2,1)}), bf16[20,80,640]{2,1,0:T(8,128)(2,1)}) %all-gather.15.cloned.1.call-update) | async-done | bytes 2048016 | tf_op jit(solution)/shard_map/all_gather | solution.py:235
  122.0 8.4 %multiply_convert_fusion.1 = bf16[1,640,1024]{1,2,0:T(8,128)(2,1)S(1)} fusion(f32[640]{0:T(1024)S(1)} %add.203, f32[640]{0:T(1024)S(1)} %mul.450, f32[1024]{0:T(1024)S(1)} %add_rsqrt_fusion.1, f32[1024]{0:T(1024)S(1)} %broadcast_multiply_fusion.5, f32[640]{0:T(1024)S(1)} %add.199, f32[1024,640]{1,0:T(8,128)} %copy-done.3), kind=kLoop, calls=%fused_computation.123 | loop fusion | flops 45875200 | bytes 3948032 | tf_op jit(solution)/shard_map/convert_element_type | solution.py:263
  137.3 8.0 %constant_dynamic-update-slice_fusion = bf16[1,3200,1024]{1,2,0:T(8,128)(2,1)} fusion(bf16[1,3200,1024]{1,2,0:T(8,128)(2,1)} %fusion.99, f32[640]{0:T(1024)S(1)} %add.203, f32[640]{0:T(1024)S(1)} %mul.450, f32[1024]{0:T(1024)S(1)} %add_rsqrt_fusion.1, f32[1024]{0:T(1024)S(1)} %broadcast_multiply_fusion.5, f32[640]{0:T(1024)S(1)} %add.199, ...), kind=kLoop, calls=%fused_computation.192 | loop fusion | flops 45875200 | bytes 3948032
  148.2 2.6 copy.61
  150.9 9.4 %fusion.74 = (f32[1024]{0:T(1024)S(1)}, f32[1024,640]{1,0:T(8,128)S(1)}) fusion(f32[640]{0:T(1024)S(1)} %add.208, bf16[3200,640]{1,0:T(8,128)(2,1)S(1)} %bitcast.261, bf16[1,3200,1024]{1,2,0:T(8,128)(2,1)} %fusion.97), kind=kOutput, calls=%fused_computation.142 | convolution fusion | flops 4195613696 | bytes 13277696 | tf_op jit(solution)/shard_map/co,rcl->rol/dot_general | solution.py:267
  162.4 12.2 %fusion.107 = f32[640,1280]{1,0:T(8,128)} fusion(bf16[1280,1024]{1,0:T(8,128)(2,1)} %bitcast.14, f32[640]{0:T(1024)S(1)} %add.212, f32[640]{0:T(1024)S(1)} %mul.461, f32[1024]{0:T(1024)S(1)} %add_rsqrt_fusion, f32[1024]{0:T(1024)S(1)} %broadcast_multiply_fusion.4, f32[640]{0:T(1024)S(1)} %add.208, f32[1024,640]{1,0:T(8,128)} %copy-done.6), kind=kOutput, calls=%fused_computation.222 | convolution fusion | flops 1723596800 | bytes 8535552 | tf_op jit(solution)/shard_map/rhl,rdl->hd/dot_general | solution.py:275
  174.6 4.5 reshape.1454
  180.9 9.4 %copy.69 = bf16[1,3200,1024]{2,1,0:T(8,128)(2,1)} copy(bf16[1,3200,1024]{1,2,0:T(8,128)(2,1)} %fusion.97) | data formatting | bytes 13107200 | tf_op jit(solution)/shard_map/concatenate | solution.py:164
  190.5 12.5 %all-gather.11.cloned.1.call-done = bf16[4,160,1280]{2,1,0:T(8,128)(2,1)} async-done(((bf16[4,80,1280]{2,1,0:T(8,128)(2,1)}), bf16[4,160,1280]{2,1,0:T(8,128)(2,1)}) %all-gather.11.cloned.1.call-update) | async-done | bytes 1638416 | tf_op jit(solution)/shard_map/all_gather | solution.py:245
  203.0 12.3 %fusion.50 = (f32[640]{0:T(1024)S(1)}, f32[1024]{0:T(1024)S(1)}, f32[1024]{0:T(1024)S(1)}, f32[640]{0:T(1024)S(1)}, f32[1,640,1024]{1,2,0:T(8,128)S(1)}) fusion(f32[1024]{0:T(1024)S(1)} %add_rsqrt_fusion, f32[1024]{0:T(1024)S(1)} %broadcast_multiply_fusion.4, f32[640]{0:T(1024)S(1)} %add.208, f32[1024,640]{1,0:T(8,128)} %copy-done.6, f32[640]{0:T(1024)S(1)} %mul.461, ...), kind=kOutput, calls=%fused_computation.89 | convolution fusion | flops 1732113152 | bytes 9531904 | tf_op jit(solution)/shard_map/hd,rdl->rhl/dot_general | solution.py:283
  218.2 7.1 %fusion.100 = f32[640,25,128]{2,0,1:T(8,128)} fusion(bf16[25,128,1024]{2,1,0:T(8,128)(2,1)S(1)} %bitcast.265, bf16[1,640,1024]{1,2,0:T(8,128)(2,1)S(1)} %get-tuple-element.55), kind=kOutput, calls=%fused_computation.180 | convolution fusion | flops 4194304000 | bytes 16056320 | tf_op jit(solution)/shard_map/rol,rkcil->okci/dot_general | solution.py:289
  225.3 17.5 %reduce-scatter.9.cloned.1.call-done.refs_0_ = f32[4,200,128]{2,1,0:T(8,128)} async-done(((f32[4,800,128]{2,1,0:T(8,128)}), f32[4,200,128]{2,1,0:T(8,128)}) %reduce-scatter.9.cloned.1.call-update) | async-done | bytes 409616 | tf_op jit(solution)/shard_map/reduce_scatter | solution.py:280
  242.9 5.9 %copy.65 = f32[1,1280,1024]{1,2,0:T(8,128)} copy(f32[1,1280,1024]{2,1,0:T(8,128)} %bitcast.259) | data formatting | bytes 10485760 | tf_op jit(solution)/shard_map/convert_element_type | solution.py:258
  248.8 2.9 convert_reduce_fusion.3
  253.1 12.3 %fusion.12 = bf16[1,1280,1024]{1,2,0:T(8,128)(2,1)} fusion(f32[1,1280,1024]{1,2,0:T(8,128)} %copy.65, bf16[640,1280]{1,0:T(8,128)(2,1)} %bitcast.277, f32[1280]{0:T(1024)S(1)} %add.216, f32[640]{0:T(1024)S(1)} %add.212, f32[640]{0:T(1024)S(1)} %mul.461, f32[1024]{0:T(1024)S(1)} %add_rsqrt_fusion, f32[1024]{0:T(1024)S(1)} %broadcast_multiply_fusion.4, ...), kind=kOutput, calls=%fused_computation.15 | convolution fusion | flops 1727528960 | bytes 12145152 | tf_op jit(solution)/shard_map/hd,rhl->rdl/dot_general | solution.py:270
  265.4 4.5 copy.66
  269.9 4.5 all-to-all-start.2
  274.5 3.2 collective-permute-start.5
  277.7 8.3 %copy.64 = bf16[5,640,640]{2,1,0:T(8,128)(2,1)} copy(bf16[5,640,640]{1,2,0:T(8,128)(2,1)} %bitcast.262) | data formatting | bytes 8192000 | tf_op jit(solution)/shard_map/transpose | solution.py:297
  293.4 16.7 %fusion.56 = (f32[640]{0:T(1024)S(1)}, f32[1024]{0:T(1024)S(1)}, f32[1024]{0:T(1024)S(1)}, f32[640]{0:T(1024)S(1)}, f32[1,640,1024]{1,2,0:T(8,128)}) fusion(f32[1024]{0:T(1024)S(1)} %add_rsqrt_fusion.1, f32[1024]{0:T(1024)S(1)} %broadcast_multiply_fusion.5, f32[640]{0:T(1024)S(1)} %add.199, f32[1024,640]{1,0:T(8,128)} %copy-done.3, f32[640]{0:T(1024)S(1)} %mul.450, ...), kind=kOutput, calls=%fused_computation.100 | convolution fusion | flops 4248695808 | bytes 15921664 | tf_op jit(solution)/shard_map/oc,rol->rcl/dot_general | solution.py:298
  310.3 3.1 fusion.55
  313.5 19.2 %multiply_reduce_fusion = (f32[1280]{0:T(1024)S(1)}, f32[1024]{0:T(1024)S(1)}, f32[1024]{0:T(1024)S(1)}, f32[1280]{0:T(1024)S(1)}, f32[1,1280,1024]{1,2,0:T(8,128)}) fusion(f32[1,1280,1024]{1,2,0:T(8,128)} %copy.65, f32[1024]{0:T(1024)S(1)} %copy-done.15, f32[1024]{0:T(1024)S(1)} %copy-done.18, f32[1280]{0:T(1024)S(1)} %copy-done.12, ...), kind=kOutput, calls=%fused_computation.21 | convolution fusion | flops 1785196032 | bytes 13471744 | tf_op jit(solution)/shard_map/dh,rhl->rdl/dot_general | solution.py:306
  333.4 5.7 %fusion.57 = f32[1280,640]{1,0:T(8,128)} fusion(bf16[1,1280,1,1,1,1,1024]{6,1,5,4,3,2,0:T(8,128)(2,1)} %fusion.6, bf16[1,640,1024]{1,2,0:T(8,128)(2,1)S(1)} %fusion.55), kind=kOutput, calls=%fused_computation.102 | convolution fusion | flops 1677721600 | bytes 7208960 | tf_op jit(solution)/shard_map/rdl,rhl->dh/dot_general | solution.py:305
  339.0 4.5 reshape.1459
  343.5 7.8 %shard_map.256 = f32[3,200,128]{2,1,0:T(8,128)} custom-call(f32[4,200,128]{2,1,0:T(8,128)} %reduce-scatter.9.cloned.1.call-done.refs_0_), custom_call_target="tpu_custom_call" | custom-call | bytes 819200 | tf_op jit(solution)/shard_map/pallas_call | solution.py:87
  353.3 19.9 %all_gather.42 = f32[4,200,128]{2,1,0:T(8,128)S(1)} all-gather(f32[1,200,128]{2,1,0:T(8,128)S(1)} %bitcast_add_fusion.4), channel_id=1, replica_groups=mesh['batch'=4,'seq'=2,'ch'=4] {'batch'}, dimensions={0}, use_global_device_ids=true | all-gather | bytes 512000 | tf_op jit(solution)/shard_map/all_gather | solution.py:338
  375.5 4.0 pad_maximum_fusion
  383.6 21.6 %shard_map.255 = f32[80,5,3,160]{3,2,1,0:T(4,128)} custom-call(f32[80,5,4,160]{3,2,1,0:T(4,128)} %reshape.1457.refs_0_), custom_call_target="tpu_custom_call" | custom-call | bytes 2048000 | tf_op jit(solution)/shard_map/pallas_call | solution.py:87
  407.9 2.7 dynamic-slice_reduce_fusion
  410.9 20.9 %all_gather.40 = f32[4,500,128]{2,1,0:T(8,128)} all-gather(f32[1,500,128]{2,1,0:T(8,128)S(1)} %add.222), channel_id=1, replica_groups=mesh['batch'=4,'seq'=2,'ch'=4] {'batch'}, dimensions={0}, use_global_device_ids=true | all-gather | bytes 1280000 | tf_op jit(solution)/shard_map/all_gather | solution.py:338
  431.9 4.9 copy.68
  436.8 8.8 %add_convert_fusion = bf16[1,1280,1024]{1,2,0:T(8,128)(2,1)} fusion(f32[1,1280,1024]{1,2,0:T(8,128)} %copy.68, f32[1,1280,1024]{1,2,0:T(8,128)} %get-tuple-element.86, f32[1,1280,1024]{1,2,0:T(8,128)} %copy.65, f32[1024]{0:T(1024)S(1)} %broadcast_multiply_fusion.6, f32[1024]{0:T(1024)S(1)} %broadcast_multiply_fusion.7, f32[1280]{0:T(1024)S(1)} %copy-done.12, ...), kind=kLoop, calls=%fused_computation.22 | loop fusion | flops 11796480 | bytes 18371584 | tf_op jit(solution)/shard_map/convert_element_type | solution.py:310
  445.6 4.8 reshape.1458
  450.4 4.5 copy.72
  454.9 4.6 all-to-all-start.3
  460.5 5.1 copy.73
  465.6 23.1 %all-to-all-done.3 = bf16[4,320,1024]{2,1,0:T(8,128)(2,1)} async-done(((bf16[4,320,1024]{2,1,0:T(8,128)(2,1)}), bf16[4,320,1024]{2,1,0:T(8,128)(2,1)}, u32[]{:S(2)}, u32[]{:S(2)}) %all-to-all-start.3) | async-done | bytes 2621472 | tf_op jit(solution)/shard_map/all_to_all | solution.py:185
  488.7 7.2 %shard_map.257 = f32[3,208,128]{2,1,0:T(8,128)} custom-call(f32[4,208,128]{2,1,0:T(8,128)} %reduce-scatter.17.cloned.1.call-done.refs_0_), custom_call_target="tpu_custom_call" | custom-call | bytes 851968 | tf_op jit(solution)/shard_map/pallas_call | solution.py:87
  497.8 14.3 %all_gather.44 = f32[4,208,128]{2,1,0:T(8,128)S(1)} all-gather(f32[1,208,128]{2,1,0:T(8,128)S(1)} %bitcast_add_fusion.3), channel_id=1, replica_groups=mesh['batch'=4,'seq'=2,'ch'=4] {'batch'}, dimensions={0}, use_global_device_ids=true | all-gather | bytes 532480 | tf_op jit(solution)/shard_map/all_gather | solution.py:338
  516.9 3.6 copy.93
  520.5 3.5 copy.94
  (163 shorter events, 67.7 us)
Async XLA Ops:
  7.2 39.7 %copy-start = (bf16[5,160,640]{2,1,0:T(8,128)(2,1)S(1)}, bf16[5,160,640]{2,1,0:T(8,128)(2,1)}, u32[]{:S(2)}) copy-start(bf16[5,160,640]{2,1,0:T(8,128)(2,1)} %param.23) | copy-start | bytes 3072004
  7.2 99.5 %all-gather.7.cloned.1.call-start = ((), (), s32[]{:S(2)}) async-start(), calls=%async_computation.10 | async-start | bytes 2457600 | tf_op jit(solution)/shard_map/all_gather | solution.py:243
  37.0 10.8 %copy-start.13 = (f32[1920]{0:T(1024)S(1)}, f32[1920]{0:T(1024)}, u32[]{:S(2)}) copy-start(f32[1920]{0:T(1024)} %concatenate.42.refs_0_) | copy-start | bytes 23044
  37.0 10.8 %copy-start.16 = (f32[4,1920]{1,0:T(4,128)S(1)}, f32[4,1920]{1,0:T(4,128)}, u32[]{:S(2)}) copy-start(f32[4,1920]{1,0:T(4,128)} %get-tuple-element.25) | copy-start | bytes 92164
  37.0 41.1 %all-to-all-start = ((bf16[4,320,1024]{2,1,0:T(8,128)(2,1)}), bf16[4,320,1024]{2,1,0:T(8,128)(2,1)}, u32[]{:S(2)}, u32[]{:S(2)}) async-start(bf16[4,320,1024]{2,1,0:T(8,128)(2,1)} %param.15), calls=%async_computation | async-start | bytes 5242880 | tf_op jit(solution)/shard_map/all_to_all | solution.py:172
  41.7 80.3 %all-gather.15.cloned.1.call-start = ((), (), s32[]{:S(2)}) async-start(), calls=%async_computation.20 | async-start | bytes 2560000 | tf_op jit(solution)/shard_map/all_gather | solution.py:235
  42.6 89.8 %collective-permute-start = (s32[1,64]{1,0:T(1,128)S(1)}, s32[1,64]{1,0:T(1,128)S(1)}, u32[]{:S(2)}, u32[]{:S(2)}) collective-permute-start(s32[1,64]{1,0:T(1,128)S(1)} %get-tuple-element.79), channel_id=1, source_target_pairs={{4,0},{5,1},{6,2},{7,3},{12,8},{13,9},{14,10},{15,11},{20,16},{21,... | collective-permute-start | bytes 776 | tf_op jit(solution)/shard_map/ppermute | solution.py:152
  43.9 88.6 %collective-permute-start.1 = (s32[1,64]{1,0:T(1,128)S(1)}, s32[1,64]{1,0:T(1,128)S(1)}, u32[]{:S(2)}, u32[]{:S(2)}) collective-permute-start(s32[1,64]{1,0:T(1,128)S(1)} %get-tuple-element.78), channel_id=1, source_target_pairs={{0,4},{1,5},{2,6},{3,7},{8,12},{9,13},{10,14},{11,15},{16,20},{17,... | collective-permute-start | bytes 776 | tf_op jit(solution)/shard_map/ppermute | solution.py:151
  48.1 42.1 %copy-start.11 = (f32[1280]{0:T(1024)}, f32[1280]{0:T(1024)S(1)}, u32[]{:S(2)}) copy-start(f32[1280]{0:T(1024)S(1)} %mul.439) | copy-start | bytes 15364
  48.2 42.0 %copy-start.19 = (f32[1280]{0:T(1024)}, f32[1280]{0:T(1024)S(1)}, u32[]{:S(2)}) copy-start(f32[1280]{0:T(1024)S(1)} %add.196) | copy-start | bytes 15364
  78.1 84.3 %all-to-all-start.1 = ((bf16[4,320,1024]{2,1,0:T(8,128)(2,1)}), bf16[4,320,1024]{2,1,0:T(8,128)(2,1)}, u32[]{:S(2)}, u32[]{:S(2)}) async-start(bf16[4,320,1024]{2,1,0:T(8,128)(2,1)} %param.29), calls=%async_computation.1 | async-start | bytes 5242880 | tf_op jit(solution)/shard_map/all_to_all | solution.py:172
  82.7 65.5 %all-gather.9.cloned.1.call-start = ((), (), s32[]{:S(2)}) async-start(), calls=%async_computation.11 | async-start | bytes 6144000 | tf_op jit(solution)/shard_map/all_gather | solution.py:244
  85.3 4.9 copy-start.14
  87.8 2.4 copy-start.17
  90.2 2.3 copy-start.2
  111.3 1.5 copy-start.3
  122.0 68.5 %reduce-scatter.7.cloned.1.call-start = ((), (), s32[]{:S(2)}) async-start(), calls=%async_computation.13 | async-start | bytes 4915200 | tf_op jit(solution)/shard_map/reduce_scatter | solution.py:279
  130.4 3.9 collective-permute-start.2
  132.6 12.7 %collective-permute-start.3 = (bf16[1,640,64]{1,2,0:T(8,128)(2,1)S(1)}, bf16[1,640,64]{1,2,0:T(8,128)(2,1)S(1)}, u32[]{:S(2)}, u32[]{:S(2)}) collective-permute-start(bf16[1,640,64]{1,2,0:T(8,128)(2,1)S(1)} %get-tuple-element.58), channel_id=1, source_target_pairs={{4,0},{5,1},{6,2},{7,3},{12,8},{13,9},{14,10},{15,11},{20,16},{21,... | collective-permute-start | bytes 245768 | tf_op jit(solution)/shard_map/ppermute | solution.py:152
  134.3 3.0 copy-start.4
  150.8 9.4 %copy-start.5 = (bf16[5,4,160,640]{3,2,1,0:T(8,128)(2,1)}, bf16[5,4,160,640]{3,2,1,0:T(8,128)(2,1)S(1)}, u32[]{:S(2)}) copy-start(bf16[5,4,160,640]{3,2,1,0:T(8,128)(2,1)S(1)} %copy.61) | copy-start | bytes 12288004
  160.2 1.6 copy-start.6
  179.1 1.0 copy-start.10
  179.1 23.9 %all-gather.11.cloned.1.call-start = ((), (), s32[]{:S(2)}) async-start(), calls=%async_computation.12 | async-start | bytes 2457600 | tf_op jit(solution)/shard_map/all_gather | solution.py:245
  180.8 62.0 %reduce-scatter.9.cloned.1.call-start = ((), (), s32[]{:S(2)}) async-start(), calls=%async_computation.14 | async-start | bytes 2048000 | tf_op jit(solution)/shard_map/reduce_scatter | solution.py:280
  190.5 102.8 %reduce-scatter.11.cloned.1.call-start = ((), (), s32[]{:S(2)}) async-start(), calls=%async_computation.15 | async-start | bytes 12288000 | tf_op jit(solution)/shard_map/reduce_scatter | solution.py:279
  203.0 12.3 %copy-start.7 = (f32[1024,640]{1,0:T(8,128)S(1)}, f32[1024,640]{1,0:T(8,128)}, u32[]{:S(2)}) copy-start(f32[1024,640]{1,0:T(8,128)} %copy-done.6) | copy-start | bytes 7864324
  215.4 2.9 copy-start.9
  248.8 4.3 copy-start.8
  251.8 34.4 %collective-permute-start.4 = (bf16[1,640,64]{1,2,0:T(8,128)(2,1)S(1)}, bf16[1,640,64]{1,2,0:T(8,128)(2,1)S(1)}, u32[]{:S(2)}, u32[]{:S(2)}) collective-permute-start(bf16[1,640,64]{1,2,0:T(8,128)(2,1)S(1)} %get-tuple-element.57), channel_id=1, source_target_pairs={{4,0},{5,1},{6,2},{7,3},{12,8},{13,9},{14,10},{15,11},{20,16},{21,... | collective-permute-start | bytes 245768 | tf_op jit(solution)/shard_map/ppermute | solution.py:152
  269.9 43.5 %all-to-all-start.2 = ((bf16[4,320,1024]{2,1,0:T(8,128)(2,1)}), bf16[4,320,1024]{2,1,0:T(8,128)(2,1)}, u32[]{:S(2)}, u32[]{:S(2)}) async-start(bf16[4,320,1024]{2,1,0:T(8,128)(2,1)} %bitcast.263), calls=%async_computation.4 | async-start | bytes 5242880 | tf_op jit(solution)/shard_map/all_to_all | solution.py:185
  274.4 105.1 %reduce-scatter.13.cloned.1.call-start = ((), (), s32[]{:S(2)}) async-start(), calls=%async_computation.16 | async-start | bytes 5120000 | tf_op jit(solution)/shard_map/reduce_scatter | solution.py:280
  274.5 15.9 %collective-permute-start.5 = (bf16[1,640,64]{1,2,0:T(8,128)(2,1)S(1)}, bf16[1,640,64]{1,2,0:T(8,128)(2,1)S(1)}, u32[]{:S(2)}, u32[]{:S(2)}) collective-permute-start(bf16[1,640,64]{1,2,0:T(8,128)(2,1)S(1)} %get-tuple-element.56), channel_id=1, source_target_pairs={{0,4},{1,5},{2,6},{3,7},{8,12},{9,13},{10,14},{11,15},{16,20},{17,... | collective-permute-start | bytes 245768 | tf_op jit(solution)/shard_map/ppermute | solution.py:151
  293.3 143.5 %reduce-scatter.15.cloned.1.call-start = ((), (), s32[]{:S(2)}) async-start(), calls=%async_computation.18 | async-start | bytes 5111808 | tf_op jit(solution)/shard_map/reduce_scatter | solution.py:279
  310.3 3.2 copy-start.12
  310.3 3.2 copy-start.15
  310.3 3.2 copy-start.18
  310.3 3.2 copy-start.20
  383.5 62.1 %all-gather.13.cloned.1.call-start = ((), (), s32[]{:S(2)}) async-start(), calls=%async_computation.17 | async-start | bytes 3096576 | tf_op jit(solution)/shard_map/all_gather | solution.py:339
  431.8 56.8 %reduce-scatter.17.cloned.1.call-start = ((), (), s32[]{:S(2)}) async-start(), calls=%async_computation.19 | async-start | bytes 2129920 | tf_op jit(solution)/shard_map/reduce_scatter | solution.py:280
  454.9 33.8 %all-to-all-start.3 = ((bf16[4,320,1024]{2,1,0:T(8,128)(2,1)}), bf16[4,320,1024]{2,1,0:T(8,128)(2,1)}, u32[]{:S(2)}, u32[]{:S(2)}) async-start(bf16[4,320,1024]{2,1,0:T(8,128)(2,1)} %bitcast.264), calls=%async_computation.7 | async-start | bytes 5242880 | tf_op jit(solution)/shard_map/all_to_all | solution.py:185
  516.9 7.0 %copy-start.1 = (bf16[5,160,640]{2,1,0:T(8,128)(2,1)S(1)}, bf16[5,160,640]{2,1,0:T(8,128)(2,1)}, u32[]{:S(2)}) copy-start(bf16[5,160,640]{2,1,0:T(8,128)(2,1)} %param.23) | copy-start | bytes 3072004
Sparse Core Ops, SparseCore 0:
  37.1 11.0 all-gather.6
  50.6 71.2 all-gather.14
  123.5 12.9 all-gather.8
  179.3 11.1 reduce-scatter.6
  191.9 11.0 all-gather.10
  205.3 37.4 reduce-scatter.8
  245.1 15.6 reduce-scatter.10
  293.4 80.1 reduce-scatter.12
  383.6 9.8 reduce-scatter.14
  432.0 9.8 all-gather.12
  444.2 38.4 reduce-scatter.16
where the time goes:
time: 540 us; the launch traced here: 531 us
  matrix products  99.6 us (18%)
  local copies, waits for them, and re-layouts  95.7 us (18%)
  waiting for transfers between devices  91.4 us (17%)
  other arithmetic  78.3 us (14%)
  blocking collectives  59.9 us (11%)
  Pallas kernels  59.8 us (11%)
  starting transfers between devices  31.3 us (6%)
  between operations  14.7 us (3%)
    pallas_call x4, Pallas kernels, exchange(): pl.pallas_call(functools.partial(_exchange_kernel, sizes, group, gather,...  59.8 us
    all_gather x3, blocking collectives, finish(): part = lax.all_gather(part, 'batch', axis=0)  55.1 us
    all_to_all x2, waiting for transfers between devices, to_positions(): x = lax.all_to_all(x, 'ch', 0, 0, tiled=True)  29.4 us
    all_to_all x2, waiting for transfers between devices, to_channels(): x = lax.all_to_all(x, 'ch', 0, 0, tiled=True)  23.1 us
    dot_general x1, matrix products, local(): jnp.einsum('dh,rhl->rdl', w_in, grad_inner, preferred_element_type=jnp.fl...  19.2 us
    reduce_scatter x3, waiting for transfers between devices, reduce_seq_batch(): return lax.psum_scatter(g, 'batch', scatter_dimension=split_dim, tiled=True)  17.5 us
    unnamed x7, other arithmetic  16.8 us
    dot_general x1, matrix products, local(): jnp.einsum('oc,rol->rcl', kernel_back, back_taps, preferred_element_type=...  16.7 us
  transfers between devices with their start and end apart: 21, of which 6 were waited for; matrix products, arithmetic and copies ran while one was open for 43% of the time, Pallas kernels for 6%

commit v1 on v0

--- a/solution.py
+++ b/solution.py
@@ -279,7 +279,7 @@
         g = lax.psum_scatter(g, "seq", scatter_dimension=split_dim, tiled=True)
         return lax.psum_scatter(g, "batch", scatter_dimension=split_dim, tiled=True)
 
-    part_outer = reduce_seq_batch(grad_w_outer.reshape(nch, hloc * dim // 128, 128), 1)
+    part_outer = reduce_seq_batch(grad_w_outer.reshape(nch, hloc, dim), 2)
     grad_hidden2 = jnp.einsum("hd,rdl->rhl", w_out, cot, preferred_element_type=jnp.float32)
     grad_normed2 = gelu_back(normed2, grad_hidden2)
     grad_norm2_gain = jnp.sum(grad_normed2 * unit2, axis=(0, 2))
@@ -347,7 +347,7 @@
     input_grad, red_conv = lax.optimization_barrier((input_grad, red_conv))
     input_grad = to_channels(input_grad, nch, q_count, rows)
     red_inner = finish(part_inner, 0, 3)
-    red_w_outer = red_outer.reshape(hloc, dim)
+    red_w_outer = jnp.moveaxis(red_outer, 0, 1).reshape(hloc, dim)
     red_w_conv = red_conv.reshape(hid, KERNEL_TAPS, hloc).transpose(1, 2, 0)
     red_inner = red_inner.reshape(-1)
     red_w_inner = red_inner[: dloc * hid].reshape(dloc, hid)

time: 540 us -> 554 us (1.026)
  local copies, waits for them, and re-layouts: 95.7 us -> 107 us
  matrix products: 99.6 us -> 89.3 us
  Pallas kernels: 59.8 us -> 68.7 us
    unnamed x11 -> x12, waiting for transfers between devices: 0.18 us -> 19 us
    reduce_scatter x3 -> x2, waiting for transfers between devices: 17.5 us -> 0.01 us  [reduce_seq_batch(): return lax.psum_scatter(g, 'batch', scatter_dimension=split_dim, tiled=True)]
    reduce_scatter x3, waiting for transfers between devices: 0.16 us -> 13.4 us  [reduce_seq_batch(): g = lax.psum_scatter(g, 'seq', scatter_dimension=split_dim, tiled=True)]
    all_gather x1, waiting for transfers between devices: 12.5 us -> 0.02 us  [local(): w_out = lax.all_gather(w_out, 'seq', axis=1, tiled=True).reshape(hid, dim)]
    pallas_call x4, Pallas kernels: 59.8 us -> 68.7 us  [exchange(): pl.pallas_call(functools.partial(_exchange_kernel, sizes, group, gather,...]
    reduce_sum x1, other arithmetic: 1.16 us -> 8.51 us  [local(): grad_b_conv = jnp.sum(grad_mixed.astype(jnp.float32), axis=(0, 2))]
    unnamed x47 -> x37, local copies, waits for them, and re-layouts: 16.3 us -> 23.5 us
    dot_general x1, matrix products: 12.2 us -> 5.8 us  [local(): jnp.einsum('rhl,rdl->hd', hidden2, cot, preferred_element_type=jnp.float32)]
  transfers between devices with their start and end apart: 21 -> 21, of which waited for: 6 -> 5; matrix products, arithmetic and copies ran while one was open for 43% -> 40% of each run, Pallas kernels for 6% -> 11%
where the time goes in v1:
time: 554 us; the launch traced here: 544 us
  local copies, waits for them, and re-layouts  107 us (19%)
  waiting for transfers between devices  91.3 us (16%)
  matrix products  89.3 us (16%)
  other arithmetic  81.9 us (15%)
  Pallas kernels  68.7 us (12%)
  blocking collectives  60.4 us (11%)
  starting transfers between devices  30.7 us (6%)
  between operations  14.9 us (3%)
    pallas_call x4, Pallas kernels, exchange(): pl.pallas_call(functools.partial(_exchange_kernel, sizes, group, gather,...  68.7 us
    all_gather x3, blocking collectives, finish(): part = lax.all_gather(part, 'batch', axis=0)  55.6 us
    all_to_all x2, waiting for transfers between devices, to_positions(): x = lax.all_to_all(x, 'ch', 0, 0, tiled=True)  24 us
    unnamed x37, local copies, waits for them, and re-layouts  23.5 us
    all_to_all x2, waiting for transfers between devices, to_channels(): x = lax.all_to_all(x, 'ch', 0, 0, tiled=True)  20.2 us
    dot_general x1, matrix products, local(): jnp.einsum('dh,rhl->rdl', w_in, grad_inner, preferred_element_type=jnp.fl...  19.3 us
    unnamed x12, waiting for transfers between devices  19 us
    dot_general x1, matrix products, local(): jnp.einsum('oc,rol->rcl', kernel_back, back_taps, preferred_element_type=...  16.8 us
  transfers between devices with their start and end apart: 21, of which 5 were waited for; matrix products, arithmetic and copies ran while one was open for 40% of the time, Pallas kernels for 11%

profile of v1, /device:TPU:0, one launch (start us, length us, event | category | flops | bytes accessed | tf_op | source)
XLA Modules:
  0.0 544.1 jit_solution(2536271234838289731)
XLA Ops:
  14.1 28.7 %shard_map.254 = (f32[4,1920]{1,0:T(4,128)}, bf16[4,160,640]{2,1,0:T(8,128)(2,1)}, bf16[4,80,1280]{2,1,0:T(8,128)(2,1)}) custom-call(f32[1920]{0:T(1024)} %concatenate.42.refs_0_, bf16[160,640]{1,0:T(8,128)(2,1)} %constant_dynamic-slice_fusion.3.refs_1_, bf16[80,1280]{1,0:T(8,128)(2,1)} %constant_dynamic-slice_fusion.2.refs_2_), custom_call_target="tpu_custom_call" | custom-call | bytes 3338240 | tf_op jit(solution)/shard_map/pallas_call | solution.py:87
  43.6 14.7 %all-gather.15.cloned.1.call-done = bf16[20,80,640]{2,1,0:T(8,128)(2,1)} async-done(((bf16[5,80,640]{2,1,0:T(8,128)(2,1)}), bf16[20,80,640]{2,1,0:T(8,128)(2,1)}) %all-gather.15.cloned.1.call-update) | async-done | bytes 2048016 | tf_op jit(solution)/shard_map/all_gather | solution.py:235
  58.4 4.7 all-to-all-start
  65.2 3.0 collective-permute-start.1
  70.0 24.0 %all-to-all-done = bf16[4,320,1024]{2,1,0:T(8,128)(2,1)} async-done(((bf16[4,320,1024]{2,1,0:T(8,128)(2,1)}), bf16[4,320,1024]{2,1,0:T(8,128)(2,1)}, u32[]{:S(2)}, u32[]{:S(2)}) %all-to-all-start) | async-done | bytes 2621472 | tf_op jit(solution)/shard_map/all_to_all | solution.py:172
  93.9 4.6 all-to-all-start.1
  107.9 14.3 %fusion.6 = bf16[1,1280,1,1,1,1,1024]{6,1,5,4,3,2,0:T(8,128)(2,1)} fusion(f32[1,1280,1,1,1,1,1024]{6,1,5,4,3,2,0:T(8,128)S(1)} %bitcast.256, f32[1280]{0:T(1024)S(1)} %add.202, f32[1280]{0:T(1024)S(1)} %mul.439, f32[1024]{0:T(1024)S(1)} %add_rsqrt_fusion.2, f32[1024]{0:T(1024)S(1)} %broadcast_multiply_fusion.8), kind=kLoop, calls=%fused_computation.8 | loop fusion | flops 90439680 | bytes 7882752 | tf_op jit(solution)/shard_map/convert_element_type | solution.py:260
  122.2 4.6 fusion.72
  127.4 7.3 %multiply_convert_fusion.1 = bf16[1,640,1024]{1,2,0:T(8,128)(2,1)S(1)} fusion(f32[640]{0:T(1024)S(1)} %add.209, f32[640]{0:T(1024)S(1)} %mul.450, f32[1024]{0:T(1024)S(1)} %add_rsqrt_fusion.1, f32[1024]{0:T(1024)S(1)} %broadcast_multiply_fusion.5, f32[640]{0:T(1024)S(1)} %add.205, f32[1024,640]{1,0:T(8,128)S(1)} %get-tuple-element.82), kind=kLoop, calls=%fused_computation.123 | loop fusion | flops 45875200 | bytes 3948032 | tf_op jit(solution)/shard_map/convert_element_type | solution.py:263
  140.6 8.0 %constant_dynamic-update-slice_fusion = bf16[1,3200,1024]{1,2,0:T(8,128)(2,1)} fusion(bf16[1,3200,1024]{1,2,0:T(8,128)(2,1)} %fusion.98, f32[640]{0:T(1024)S(1)} %add.209, f32[640]{0:T(1024)S(1)} %mul.450, f32[1024]{0:T(1024)S(1)} %add_rsqrt_fusion.1, f32[1024]{0:T(1024)S(1)} %broadcast_multiply_fusion.5, f32[640]{0:T(1024)S(1)} %add.205, ...), kind=kLoop, calls=%fused_computation.191 | loop fusion | flops 45875200 | bytes 3948032
  154.1 9.2 %fusion.74 = (f32[1024]{0:T(1024)S(1)}, f32[1024,640]{1,0:T(8,128)S(1)}) fusion(f32[640]{0:T(1024)S(1)} %add.214, bf16[3200,640]{1,0:T(8,128)(2,1)S(1)} %bitcast.259, bf16[1,3200,1024]{1,2,0:T(8,128)(2,1)} %fusion.96), kind=kOutput, calls=%fused_computation.142 | convolution fusion | flops 4195613696 | bytes 13277696 | tf_op jit(solution)/shard_map/co,rcl->rol/dot_general | solution.py:267
  165.4 12.1 %fusion.50 = (f32[640]{0:T(1024)S(1)}, f32[1024]{0:T(1024)S(1)}, f32[1024]{0:T(1024)S(1)}, f32[640]{0:T(1024)S(1)}, f32[1,640,1024]{1,2,0:T(8,128)S(1)}) fusion(f32[1024]{0:T(1024)S(1)} %add_rsqrt_fusion, f32[1024]{0:T(1024)S(1)} %broadcast_multiply_fusion.4, f32[640]{0:T(1024)S(1)} %add.214, f32[1024,640]{1,0:T(8,128)} %copy-done.5, f32[640]{0:T(1024)S(1)} %mul.461, ...), kind=kOutput, calls=%fused_computation.89 | convolution fusion | flops 1732113152 | bytes 9531904 | tf_op jit(solution)/shard_map/hd,rdl->rhl/dot_general | solution.py:283
  177.5 8.5 %convert_reduce_fusion.1 = (f32[640]{0:T(1024)S(1)}, bf16[1,640,1024]{1,2,0:T(8,128)(2,1)S(1)}, bf16[1,640,1024]{1,2,0:T(8,128)(2,1)}) fusion(f32[1024]{0:T(1024)S(1)} %get-tuple-element.88, f32[1024]{0:T(1024)S(1)} %add_rsqrt_fusion, f32[1024]{0:T(1024)S(1)} %broadcast_multiply_fusion.4, f32[640]{0:T(1024)S(1)} %add.214, f32[1024,640]{1,0:T(8,128)S(1)} %copy-done.6, ...), kind=kLoop, calls=%fused_computation.107 | loop fusion | flops 51117440 | bytes 7890944 | tf_op jit(solution)/shard_map/reduce_sum | solution.py:288
  188.5 5.8 %fusion.114 = f32[4,160,1280]{2,1,0:T(8,128)} fusion(bf16[4,160,1024]{2,1,0:T(8,128)(2,1)} %bitcast.274, bf16[1280,1024,1]{1,0,2:T(8,128)(2,1)} %bitcast.28), kind=kOutput, calls=%fused_computation.229 | convolution fusion | flops 1677721600 | bytes 7208960 | tf_op jit(solution)/shard_map/rhl,rdl->hd/dot_general | solution.py:275
  194.3 13.4 %reduce-scatter.9.cloned.1.call-done = f32[4,160,640]{2,1,0:T(8,128)} async-done(((f32[4,160,1280]{2,1,0:T(8,128)}), f32[4,160,640]{2,1,0:T(8,128)}) %reduce-scatter.9.cloned.1.call-update) | async-done | bytes 1638416 | tf_op jit(solution)/shard_map/reduce_scatter | solution.py:279
  207.7 3.8 copy.83
  211.5 3.9 reshape.1498
  215.4 9.6 %copy.74 = bf16[1,3200,1024]{2,1,0:T(8,128)(2,1)} copy(bf16[1,3200,1024]{1,2,0:T(8,128)(2,1)} %fusion.96) | data formatting | bytes 13107200 | tf_op jit(solution)/shard_map/concatenate | solution.py:164
  225.0 9.1 %fusion.99 = f32[640,25,128]{2,0,1:T(8,128)} fusion(bf16[25,128,1024]{2,1,0:T(8,128)(2,1)} %bitcast.264, bf16[1,640,1024]{1,2,0:T(8,128)(2,1)S(1)} %get-tuple-element.55), kind=kOutput, calls=%fused_computation.179 | convolution fusion | flops 4194304000 | bytes 16056320 | tf_op jit(solution)/shard_map/rol,rkcil->okci/dot_general | solution.py:289
  234.1 18.8 %reduce-scatter.19.cloned.1.call-done = f32[160,640]{1,0:T(8,128)} async-done(((f32[640,640]{1,0:T(8,128)}), f32[160,640]{1,0:T(8,128)}) %reduce-scatter.19.cloned.1.call-update) | async-done | bytes 409616
  255.7 5.9 %copy.70 = f32[1,1280,1024]{1,2,0:T(8,128)} copy(f32[1,1280,1024]{2,1,0:T(8,128)} %bitcast.257) | data formatting | bytes 10485760 | tf_op jit(solution)/shard_map/convert_element_type | solution.py:258
  265.6 3.0 collective-permute-start.5
  268.6 6.7 %fusion.12 = bf16[1,1280,1024]{1,2,0:T(8,128)(2,1)} fusion(f32[1,1280,1024]{1,2,0:T(8,128)} %copy.70, bf16[640,1280]{1,0:T(8,128)(2,1)S(1)} %bitcast.279, f32[1280]{0:T(1024)S(1)} %add.222, bf16[1,640,1024]{1,2,0:T(8,128)(2,1)S(1)} %copy-done.7), kind=kOutput, calls=%fused_computation.15 | convolution fusion | flops 1681653760 | bytes 10818560 | tf_op jit(solution)/shard_map/hd,rhl->rdl/dot_general | solution.py:270
  275.3 7.9 %copy.68 = bf16[5,640,640]{2,1,0:T(8,128)(2,1)} copy(bf16[5,640,640]{1,2,0:T(8,128)(2,1)} %bitcast.260) | data formatting | bytes 8192000 | tf_op jit(solution)/shard_map/transpose | solution.py:297
  283.2 4.5 copy.71
  287.6 4.6 all-to-all-start.2
  299.8 16.8 %fusion.56 = (f32[640]{0:T(1024)S(1)}, f32[1024]{0:T(1024)S(1)}, f32[1024]{0:T(1024)S(1)}, f32[640]{0:T(1024)S(1)}, f32[1,640,1024]{1,2,0:T(8,128)}) fusion(f32[1024]{0:T(1024)S(1)} %add_rsqrt_fusion.1, f32[1024]{0:T(1024)S(1)} %broadcast_multiply_fusion.5, f32[640]{0:T(1024)S(1)} %add.205, f32[1024,640]{1,0:T(8,128)} %copy-done.3, f32[640]{0:T(1024)S(1)} %mul.450, ...), kind=kOutput, calls=%fused_computation.100 | convolution fusion | flops 4248695808 | bytes 15921664 | tf_op jit(solution)/shard_map/oc,rol->rcl/dot_general | solution.py:298
  316.8 3.1 fusion.55
  319.9 10.8 %shard_map.256 = f32[3,160,160]{2,1,0:T(8,128)} custom-call(f32[4,160,160]{2,1,0:T(8,128)} %copy.84.refs_0_), custom_call_target="tpu_custom_call" | custom-call | bytes 819200 | tf_op jit(solution)/shard_map/pallas_call | solution.py:87
  330.8 19.3 %multiply_reduce_fusion = (f32[1280]{0:T(1024)S(1)}, f32[1024]{0:T(1024)S(1)}, f32[1024]{0:T(1024)S(1)}, f32[1280]{0:T(1024)S(1)}, f32[1,1280,1024]{1,2,0:T(8,128)}) fusion(f32[1,1280,1024]{1,2,0:T(8,128)} %copy.70, f32[1024]{0:T(1024)S(1)} %broadcast_multiply_fusion.8, f32[1024]{0:T(1024)S(1)} %add_rsqrt_fusion.2, f32[1280]{0:T(1024)S(1)} %mul.439, ...), kind=kOutput, calls=%fused_computation.21 | convolution fusion | flops 1785196032 | bytes 13471744 | tf_op jit(solution)/shard_map/dh,rhl->rdl/dot_general | solution.py:306
  350.7 5.8 %fusion.57 = f32[1280,640]{1,0:T(8,128)} fusion(bf16[1,1280,1,1,1,1,1024]{6,1,5,4,3,2,0:T(8,128)(2,1)} %fusion.6, bf16[1,640,1024]{1,2,0:T(8,128)(2,1)S(1)} %fusion.55), kind=kOutput, calls=%fused_computation.102 | convolution fusion | flops 1677721600 | bytes 7208960 | tf_op jit(solution)/shard_map/rdl,rhl->dh/dot_general | solution.py:305
  356.4 4.6 reshape.1477
  362.3 19.8 %all_gather.41 = f32[4,200,128]{2,1,0:T(8,128)S(1)} all-gather(f32[1,200,128]{2,1,0:T(8,128)S(1)} %add.229), channel_id=1, replica_groups=mesh['batch'=4,'seq'=2,'ch'=4] {'batch'}, dimensions={0}, use_global_device_ids=true | all-gather | bytes 512000 | tf_op jit(solution)/shard_map/all_gather | solution.py:338
  385.0 4.0 pad_maximum_fusion
  391.6 3.3 reshape.1475.refs_0_
  395.0 21.9 %shard_map.255 = f32[80,5,3,160]{3,2,1,0:T(4,128)} custom-call(f32[80,5,4,160]{3,2,1,0:T(4,128)} %reshape.1475.refs_0_), custom_call_target="tpu_custom_call" | custom-call | bytes 2048000 | tf_op jit(solution)/shard_map/pallas_call | solution.py:87
  422.6 21.4 %all_gather.39 = f32[4,500,128]{2,1,0:T(8,128)} all-gather(f32[1,500,128]{2,1,0:T(8,128)S(1)} %add.228), channel_id=1, replica_groups=mesh['batch'=4,'seq'=2,'ch'=4] {'batch'}, dimensions={0}, use_global_device_ids=true | all-gather | bytes 1280000 | tf_op jit(solution)/shard_map/all_gather | solution.py:338
  444.1 4.9 copy.73
  449.0 8.8 %add_convert_fusion = bf16[1,1280,1024]{1,2,0:T(8,128)(2,1)} fusion(f32[1,1280,1024]{1,2,0:T(8,128)} %copy.73, f32[1,1280,1024]{1,2,0:T(8,128)} %get-tuple-element.87, f32[1,1280,1024]{1,2,0:T(8,128)} %copy.70, f32[1024]{0:T(1024)S(1)} %broadcast_multiply_fusion.6, f32[1024]{0:T(1024)S(1)} %broadcast_multiply_fusion.7, f32[1280]{0:T(1024)S(1)} %mul.439, ...), kind=kLoop, calls=%fused_computation.22 | loop fusion | flops 11796480 | bytes 18371584 | tf_op jit(solution)/shard_map/convert_element_type | solution.py:310
  457.8 4.8 reshape.1476
  462.5 4.5 copy.77
  467.1 4.8 all-to-all-start.3
  476.5 5.1 copy.78
  481.6 20.1 %all-to-all-done.3 = bf16[4,320,1024]{2,1,0:T(8,128)(2,1)} async-done(((bf16[4,320,1024]{2,1,0:T(8,128)(2,1)}), bf16[4,320,1024]{2,1,0:T(8,128)(2,1)}, u32[]{:S(2)}, u32[]{:S(2)}) %all-to-all-start.3) | async-done | bytes 2621472 | tf_op jit(solution)/shard_map/all_to_all | solution.py:185
  501.8 7.2 %shard_map.257 = f32[3,208,128]{2,1,0:T(8,128)} custom-call(f32[4,208,128]{2,1,0:T(8,128)} %reduce-scatter.17.cloned.1.call-done.refs_0_), custom_call_target="tpu_custom_call" | custom-call | bytes 851968 | tf_op jit(solution)/shard_map/pallas_call | solution.py:87
  510.9 14.4 %all_gather.43 = f32[4,208,128]{2,1,0:T(8,128)S(1)} all-gather(f32[1,208,128]{2,1,0:T(8,128)S(1)} %bitcast_add_fusion.3), channel_id=1, replica_groups=mesh['batch'=4,'seq'=2,'ch'=4] {'batch'}, dimensions={0}, use_global_device_ids=true | all-gather | bytes 532480 | tf_op jit(solution)/shard_map/all_gather | solution.py:338
  530.1 3.6 copy.101
  533.7 3.5 copy.102
  (158 shorter events, 76.3 us)
Async XLA Ops:
  7.2 1.2 copy-start
  7.2 35.6 %copy-start.9 = (bf16[320,640]{1,0:T(8,128)(2,1)S(1)}, bf16[320,640]{1,0:T(8,128)(2,1)}, u32[]{:S(2)}) copy-start(bf16[320,640]{1,0:T(8,128)(2,1)} %param.19) | copy-start | bytes 1228804
  7.2 51.1 %all-gather.15.cloned.1.call-start = ((), (), s32[]{:S(2)}) async-start(), calls=%async_computation.19 | async-start | bytes 2560000 | tf_op jit(solution)/shard_map/all_gather | solution.py:235
  9.3 112.9 %all-gather.7.cloned.1.call-start = ((), (), s32[]{:S(2)}) async-start(), calls=%async_computation.10 | async-start | bytes 2457600 | tf_op jit(solution)/shard_map/all_gather | solution.py:243
  43.6 107.8 %all-gather.9.cloned.1.call-start = ((), (), s32[]{:S(2)}) async-start(), calls=%async_computation.11 | async-start | bytes 6144000 | tf_op jit(solution)/shard_map/all_gather | solution.py:244
  58.4 9.9 %copy-start.10 = (bf16[160,1280]{1,0:T(8,128)(2,1)S(1)}, bf16[160,1280]{1,0:T(8,128)(2,1)}, u32[]{:S(2)}) copy-start(bf16[160,1280]{1,0:T(8,128)(2,1)} %param.27) | copy-start | bytes 1228804
  58.4 10.6 %copy-start.11 = (f32[1920]{0:T(1024)S(1)}, f32[1920]{0:T(1024)}, u32[]{:S(2)}) copy-start(f32[1920]{0:T(1024)} %concatenate.42.refs_0_) | copy-start | bytes 23044
  58.4 10.6 %copy-start.12 = (f32[4,1920]{1,0:T(4,128)S(1)}, f32[4,1920]{1,0:T(4,128)}, u32[]{:S(2)}) copy-start(f32[4,1920]{1,0:T(4,128)} %get-tuple-element.25) | copy-start | bytes 92164
  58.4 35.5 %all-to-all-start = ((bf16[4,320,1024]{2,1,0:T(8,128)(2,1)}), bf16[4,320,1024]{2,1,0:T(8,128)(2,1)}, u32[]{:S(2)}, u32[]{:S(2)}) async-start(bf16[4,320,1024]{2,1,0:T(8,128)(2,1)} %param.15), calls=%async_computation | async-start | bytes 5242880 | tf_op jit(solution)/shard_map/all_to_all | solution.py:172
  63.1 102.3 %all-gather.11.cloned.1.call-start = ((), (), s32[]{:S(2)}) async-start(), calls=%async_computation.12 | async-start | bytes 2457600 | tf_op jit(solution)/shard_map/all_gather | solution.py:245
  64.0 72.1 %collective-permute-start = (s32[1,64]{1,0:T(1,128)S(1)}, s32[1,64]{1,0:T(1,128)S(1)}, u32[]{:S(2)}, u32[]{:S(2)}) collective-permute-start(s32[1,64]{1,0:T(1,128)S(1)} %get-tuple-element.80), channel_id=1, source_target_pairs={{4,0},{5,1},{6,2},{7,3},{12,8},{13,9},{14,10},{15,11},{20,16},{21,... | collective-permute-start | bytes 776 | tf_op jit(solution)/shard_map/ppermute | solution.py:152
  65.2 70.8 %collective-permute-start.1 = (s32[1,64]{1,0:T(1,128)S(1)}, s32[1,64]{1,0:T(1,128)S(1)}, u32[]{:S(2)}, u32[]{:S(2)}) collective-permute-start(s32[1,64]{1,0:T(1,128)S(1)} %get-tuple-element.79), channel_id=1, source_target_pairs={{0,4},{1,5},{2,6},{3,7},{8,12},{9,13},{10,14},{11,15},{16,20},{17,... | collective-permute-start | bytes 776 | tf_op jit(solution)/shard_map/ppermute | solution.py:151
  93.9 71.4 %all-to-all-start.1 = ((bf16[4,320,1024]{2,1,0:T(8,128)(2,1)}), bf16[4,320,1024]{2,1,0:T(8,128)(2,1)}, u32[]{:S(2)}, u32[]{:S(2)}) async-start(bf16[4,320,1024]{2,1,0:T(8,128)(2,1)} %param.29), calls=%async_computation.1 | async-start | bytes 5242880 | tf_op jit(solution)/shard_map/all_to_all | solution.py:172
  98.5 109.2 %reduce-scatter.9.cloned.1.call-start = ((), (), s32[]{:S(2)}) async-start(), calls=%async_computation.13 | async-start | bytes 4915200 | tf_op jit(solution)/shard_map/reduce_scatter | solution.py:279
  105.6 2.3 copy-start.2
  126.8 13.8 %copy-start.3 = (f32[1024,640]{1,0:T(8,128)}, f32[1024,640]{1,0:T(8,128)S(1)}, u32[]{:S(2)}) copy-start(f32[1024,640]{1,0:T(8,128)S(1)} %get-tuple-element.82) | copy-start | bytes 7864324
  134.7 3.0 collective-permute-start.2
  136.2 12.4 %collective-permute-start.3 = (bf16[1,640,64]{1,2,0:T(8,128)(2,1)S(1)}, bf16[1,640,64]{1,2,0:T(8,128)(2,1)S(1)}, u32[]{:S(2)}, u32[]{:S(2)}) collective-permute-start(bf16[1,640,64]{1,2,0:T(8,128)(2,1)S(1)} %get-tuple-element.59), channel_id=1, source_target_pairs={{4,0},{5,1},{6,2},{7,3},{12,8},{13,9},{14,10},{15,11},{20,16},{21,... | collective-permute-start | bytes 245768 | tf_op jit(solution)/shard_map/ppermute | solution.py:152
  154.0 9.2 %copy-start.4 = (bf16[5,4,160,640]{3,2,1,0:T(8,128)(2,1)}, bf16[5,4,160,640]{3,2,1,0:T(8,128)(2,1)S(1)}, u32[]{:S(2)}) copy-start(bf16[5,4,160,640]{3,2,1,0:T(8,128)(2,1)S(1)} %copy.65) | copy-start | bytes 12288004
  163.3 1.5 copy-start.5
  165.4 12.1 %copy-start.6 = (f32[1024,640]{1,0:T(8,128)S(1)}, f32[1024,640]{1,0:T(8,128)}, u32[]{:S(2)}) copy-start(f32[1024,640]{1,0:T(8,128)} %copy-done.5) | copy-start | bytes 7864324
  194.3 58.7 %reduce-scatter.19.cloned.1.call-start = ((), (), s32[]{:S(2)}) async-start(), calls=%async_computation.20 | async-start | bytes 2048000
  215.4 84.4 %reduce-scatter.11.cloned.1.call-start = ((), (), s32[]{:S(2)}) async-start(), calls=%async_computation.14 | async-start | bytes 12288000 | tf_op jit(solution)/shard_map/reduce_scatter | solution.py:279
  261.6 7.0 %copy-start.7 = (bf16[1,640,1024]{1,2,0:T(8,128)(2,1)S(1)}, bf16[1,640,1024]{1,2,0:T(8,128)(2,1)}, u32[]{:S(2)}) copy-start(bf16[1,640,1024]{1,2,0:T(8,128)(2,1)} %get-tuple-element.56) | copy-start | bytes 3932164
  261.6 7.0 %copy-start.13 = (bf16[4,160,1280]{2,1,0:T(8,128)(2,1)S(1)}, bf16[4,160,1280]{2,1,0:T(8,128)(2,1)}, u32[]{:S(2)}) copy-start(bf16[4,160,1280]{2,1,0:T(8,128)(2,1)} %all-gather.11.cloned.1.call-done) | copy-start | bytes 4915204
  264.3 28.4 %collective-permute-start.4 = (bf16[1,640,64]{1,2,0:T(8,128)(2,1)S(1)}, bf16[1,640,64]{1,2,0:T(8,128)(2,1)S(1)}, u32[]{:S(2)}, u32[]{:S(2)}) collective-permute-start(bf16[1,640,64]{1,2,0:T(8,128)(2,1)S(1)} %get-tuple-element.58), channel_id=1, source_target_pairs={{4,0},{5,1},{6,2},{7,3},{12,8},{13,9},{14,10},{15,11},{20,16},{21,... | collective-permute-start | bytes 245768 | tf_op jit(solution)/shard_map/ppermute | solution.py:152
  265.6 31.3 %collective-permute-start.5 = (bf16[1,640,64]{1,2,0:T(8,128)(2,1)S(1)}, bf16[1,640,64]{1,2,0:T(8,128)(2,1)S(1)}, u32[]{:S(2)}, u32[]{:S(2)}) collective-permute-start(bf16[1,640,64]{1,2,0:T(8,128)(2,1)S(1)} %get-tuple-element.57), channel_id=1, source_target_pairs={{0,4},{1,5},{2,6},{3,7},{8,12},{9,13},{10,14},{11,15},{16,20},{17,... | collective-permute-start | bytes 245768 | tf_op jit(solution)/shard_map/ppermute | solution.py:151
  287.6 43.1 %all-to-all-start.2 = ((bf16[4,320,1024]{2,1,0:T(8,128)(2,1)}), bf16[4,320,1024]{2,1,0:T(8,128)(2,1)}, u32[]{:S(2)}, u32[]{:S(2)}) async-start(bf16[4,320,1024]{2,1,0:T(8,128)(2,1)} %bitcast.261), calls=%async_computation.3 | async-start | bytes 5242880 | tf_op jit(solution)/shard_map/all_to_all | solution.py:185
  292.2 96.8 %reduce-scatter.13.cloned.1.call-start = ((), (), s32[]{:S(2)}) async-start(), calls=%async_computation.15 | async-start | bytes 5120000 | tf_op jit(solution)/shard_map/reduce_scatter | solution.py:280
  299.8 149.2 %reduce-scatter.15.cloned.1.call-start = ((), (), s32[]{:S(2)}) async-start(), calls=%async_computation.17 | async-start | bytes 5111808 | tf_op jit(solution)/shard_map/reduce_scatter | solution.py:279
  356.4 4.6 copy-start.8
  395.0 62.8 %all-gather.13.cloned.1.call-start = ((), (), s32[]{:S(2)}) async-start(), calls=%async_computation.16 | async-start | bytes 3096576 | tf_op jit(solution)/shard_map/all_gather | solution.py:339
  444.0 57.7 %reduce-scatter.17.cloned.1.call-start = ((), (), s32[]{:S(2)}) async-start(), calls=%async_computation.18 | async-start | bytes 2129920 | tf_op jit(solution)/shard_map/reduce_scatter | solution.py:280
  467.1 34.7 %all-to-all-start.3 = ((bf16[4,320,1024]{2,1,0:T(8,128)(2,1)}), bf16[4,320,1024]{2,1,0:T(8,128)(2,1)}, u32[]{:S(2)}, u32[]{:S(2)}) async-start(bf16[4,320,1024]{2,1,0:T(8,128)(2,1)} %bitcast.262), calls=%async_computation.6 | async-start | bytes 5242880 | tf_op jit(solution)/shard_map/all_to_all | solution.py:185
  530.1 7.0 %copy-start.1 = (bf16[5,160,640]{2,1,0:T(8,128)(2,1)S(1)}, bf16[5,160,640]{2,1,0:T(8,128)(2,1)}, u32[]{:S(2)}) copy-start(bf16[5,160,640]{2,1,0:T(8,128)(2,1)} %param.23) | copy-start | bytes 3072004
Sparse Core Ops, SparseCore 0:
  10.5 47.8 all-gather.14
  59.9 9.9 all-gather.6
  71.4 14.6 all-gather.8
  87.5 11.0 all-gather.10
  194.4 13.2 reduce-scatter.8
  215.5 37.4 reduce-scatter.18
  255.7 15.7 reduce-scatter.10
  299.9 81.8 reduce-scatter.12
  395.1 10.5 reduce-scatter.14
  444.1 9.5 all-gather.12
  456.2 38.4 reduce-scatter.16

commit v2 on v0

--- a/solution.py
+++ b/solution.py
@@ -231,8 +231,7 @@
         lax.dynamic_slice_in_dim(w_conv, sidx * (hloc // seqs), hloc // seqs, 1),
         lax.dynamic_slice_in_dim(w_outer, sidx * (hloc // seqs), hloc // seqs, 0),
     ]
-    small_all, w_in, w_out = exchange([jnp.concatenate(smalls), halves[0], halves[2]], ("ch",), 0, gather=True)
-    w_cv = lax.all_gather(halves[1], "ch", axis=0)
+    small_all, w_in, w_cv, w_out = exchange([jnp.concatenate(smalls)] + halves, ("ch",), 0, gather=True)
     cut = 0
     full = []
     for v in smalls:

time: 540 us -> 532 us (0.985)
  Pallas kernels: 59.8 us -> 81.5 us
  waiting for transfers between devices: 91.4 us -> 78.6 us
  other arithmetic: 78.3 us -> 69.2 us
  local copies, waits for them, and re-layouts: 95.7 us -> 90.1 us
    pallas_call x4, Pallas kernels: 59.8 us -> 81.5 us  [exchange(): pl.pallas_call(functools.partial(_exchange_kernel, sizes, group, gather,...]
    all_gather x1 -> x0, waiting for transfers between devices: 8.56 us -> none  [local(): w_cv = lax.all_gather(halves[1], 'ch', axis=0)]
    all_to_all x2, waiting for transfers between devices: 29.4 us -> 22.8 us  [to_positions(): x = lax.all_to_all(x, 'ch', 0, 0, tiled=True)]
    unnamed x47 -> x49, local copies, waits for them, and re-layouts: 16.3 us -> 12.2 us
  transfers between devices with their start and end apart: 21 -> 20, of which waited for: 6 -> 5; matrix products, arithmetic and copies ran while one was open for 43% -> 41% of each run, Pallas kernels for 6% -> 6%
where the time goes in v2:
time: 532 us; the launch traced here: 523 us
  matrix products  98.8 us (19%)
  local copies, waits for them, and re-layouts  90.1 us (17%)
  Pallas kernels  81.5 us (15%)
  waiting for transfers between devices  78.6 us (15%)
  other arithmetic  69.2 us (13%)
  blocking collectives  61.3 us (12%)
  starting transfers between devices  28.8 us (5%)
  between operations  15 us (3%)
    pallas_call x4, Pallas kernels, exchange(): pl.pallas_call(functools.partial(_exchange_kernel, sizes, group, gather,...  81.5 us
    all_gather x3, blocking collectives, finish(): part = lax.all_gather(part, 'batch', axis=0)  56.4 us
    all_to_all x2, waiting for transfers between devices, to_channels(): x = lax.all_to_all(x, 'ch', 0, 0, tiled=True)  23.7 us
    all_to_all x2, waiting for transfers between devices, to_positions(): x = lax.all_to_all(x, 'ch', 0, 0, tiled=True)  22.8 us
    dot_general x1, matrix products, local(): jnp.einsum('dh,rhl->rdl', w_in, grad_inner, preferred_element_type=jnp.fl...  19.4 us
    reduce_scatter x3, waiting for transfers between devices, reduce_seq_batch(): return lax.psum_scatter(g, 'batch', scatter_dimension=split_dim, tiled=True)  17.2 us
    unnamed x7, other arithmetic  16.8 us
    dot_general x1, matrix products, local(): jnp.einsum('oc,rol->rcl', kernel_back, back_taps, preferred_element_type=...  16.5 us
  transfers between devices with their start and end apart: 20, of which 5 were waited for; matrix products, arithmetic and copies ran while one was open for 41% of the time, Pallas kernels for 6%

profile of v2, /device:TPU:0, one launch (start us, length us, event | category | flops | bytes accessed | tf_op | source)
XLA Modules:
  0.0 523.2 jit_solution(7443677360183058182)
XLA Ops:
  13.9 45.3 %shard_map.254 = (f32[4,1920]{1,0:T(4,128)}, bf16[4,160,640]{2,1,0:T(8,128)(2,1)}, bf16[4,5,80,640]{3,2,1,0:T(8,128)(2,1)}, bf16[4,80,1280]{2,1,0:T(8,128)(2,1)}) custom-call(f32[1920]{0:T(1024)} %concatenate.42.refs_0_, bf16[160,640]{1,0:T(8,128)(2,1)} %constant_dynamic-slice_fusion.2.refs_1_, bf16[5,80,640]{2,1,0:T(8,128)(2,1)} %constant_dynamic-slice_fusion.1.refs_2_, ...), custom_call_target="tpu_custom_call" | custom-call | bytes 7434240 | tf_op jit(solution)/shard_map/pallas_call | solution.py:87
  59.9 3.7 all-to-all-start
  65.8 3.0 collective-permute-start.1
  71.7 22.8 %all-to-all-done = bf16[4,320,1024]{2,1,0:T(8,128)(2,1)S(1)} async-done(((bf16[4,320,1024]{2,1,0:T(8,128)(2,1)}), bf16[4,320,1024]{2,1,0:T(8,128)(2,1)S(1)}, u32[]{:S(2)}, u32[]{:S(2)}) %all-to-all-start) | async-done | bytes 2621472 | tf_op jit(solution)/shard_map/all_to_all | solution.py:172
  94.4 4.6 all-to-all-start.1
  103.2 13.7 %fusion.6 = bf16[1,1280,1,1,1,1,1024]{6,1,5,4,3,2,0:T(8,128)(2,1)S(1)} fusion(f32[1,1280,1,1,1,1,1024]{6,1,5,4,3,2,0:T(8,128)S(1)} %bitcast.259, f32[1280]{0:T(1024)S(1)} %add.198, f32[1280]{0:T(1024)S(1)} %mul.439, f32[1024]{0:T(1024)S(1)} %add_rsqrt_fusion.2, f32[1024]{0:T(1024)S(1)} %broadcast_multiply_fusion.8), kind=kLoop, calls=%fused_computation.8 | loop fusion | flops 90439680 | bytes 7882752 | tf_op jit(solution)/shard_map/convert_element_type | solution.py:259
  116.9 4.7 fusion.72
  122.3 7.3 %multiply_convert_fusion.1 = bf16[1,640,1024]{1,2,0:T(8,128)(2,1)S(1)} fusion(f32[640]{0:T(1024)S(1)} %add.205, f32[640]{0:T(1024)S(1)} %mul.450, f32[1024]{0:T(1024)S(1)} %add_rsqrt_fusion.1, f32[1024]{0:T(1024)S(1)} %broadcast_multiply_fusion.5, f32[640]{0:T(1024)S(1)} %add.201, f32[1024,640]{1,0:T(8,128)S(1)} %get-tuple-element.83), kind=kLoop, calls=%fused_computation.123 | loop fusion | flops 45875200 | bytes 3948032 | tf_op jit(solution)/shard_map/convert_element_type | solution.py:262
  135.8 8.0 %constant_dynamic-update-slice_fusion = bf16[1,3200,1024]{1,2,0:T(8,128)(2,1)} fusion(bf16[1,3200,1024]{1,2,0:T(8,128)(2,1)} %fusion.99, f32[640]{0:T(1024)S(1)} %add.205, f32[640]{0:T(1024)S(1)} %mul.450, f32[1024]{0:T(1024)S(1)} %add_rsqrt_fusion.1, f32[1024]{0:T(1024)S(1)} %broadcast_multiply_fusion.5, f32[640]{0:T(1024)S(1)} %add.201, ...), kind=kLoop, calls=%fused_computation.193 | loop fusion | flops 45875200 | bytes 3948032
  146.7 2.6 copy.50
  149.4 9.4 %fusion.74 = (f32[1024]{0:T(1024)S(1)}, f32[1024,640]{1,0:T(8,128)S(1)}) fusion(f32[640]{0:T(1024)S(1)} %add.210, bf16[3200,640]{1,0:T(8,128)(2,1)S(1)} %bitcast.262, bf16[1,3200,1024]{1,2,0:T(8,128)(2,1)} %fusion.97), kind=kOutput, calls=%fused_computation.142 | convolution fusion | flops 4195613696 | bytes 13277696 | tf_op jit(solution)/shard_map/co,rcl->rol/dot_general | solution.py:266
  159.3 11.8 %fusion.107 = f32[640,1280]{1,0:T(8,128)} fusion(bf16[1280,1024]{1,0:T(8,128)(2,1)} %bitcast.14, f32[640]{0:T(1024)S(1)} %add.214, f32[640]{0:T(1024)S(1)} %mul.461, f32[1024]{0:T(1024)S(1)} %add_rsqrt_fusion, f32[1024]{0:T(1024)S(1)} %broadcast_multiply_fusion.4, f32[640]{0:T(1024)S(1)} %add.210, f32[1024,640]{1,0:T(8,128)S(1)} %get-tuple-element.85), kind=kOutput, calls=%fused_computation.223 | convolution fusion | flops 1723596800 | bytes 8535552 | tf_op jit(solution)/shard_map/rhl,rdl->hd/dot_general | solution.py:274
  171.1 4.5 reshape.1454
  177.3 9.7 %copy.58 = bf16[1,3200,1024]{2,1,0:T(8,128)(2,1)} copy(bf16[1,3200,1024]{1,2,0:T(8,128)(2,1)} %fusion.97) | data formatting | bytes 13107200 | tf_op jit(solution)/shard_map/concatenate | solution.py:164
  189.3 12.5 %all-gather.9.cloned.1.call-done = bf16[4,160,1280]{2,1,0:T(8,128)(2,1)} async-done(((bf16[4,80,1280]{2,1,0:T(8,128)(2,1)}), bf16[4,160,1280]{2,1,0:T(8,128)(2,1)}) %all-gather.9.cloned.1.call-update) | async-done | bytes 1638416 | tf_op jit(solution)/shard_map/all_gather | solution.py:244
  201.8 11.8 %fusion.50 = (f32[640]{0:T(1024)S(1)}, f32[1024]{0:T(1024)S(1)}, f32[1024]{0:T(1024)S(1)}, f32[640]{0:T(1024)S(1)}, f32[1,640,1024]{1,2,0:T(8,128)S(1)}) fusion(f32[1024]{0:T(1024)S(1)} %add_rsqrt_fusion, f32[1024]{0:T(1024)S(1)} %broadcast_multiply_fusion.4, f32[640]{0:T(1024)S(1)} %add.210, f32[1024,640]{1,0:T(8,128)S(1)} %get-tuple-element.85, ...), kind=kOutput, calls=%fused_computation.89 | convolution fusion | flops 1732113152 | bytes 9531904 | tf_op jit(solution)/shard_map/hd,rdl->rhl/dot_general | solution.py:282
  213.6 2.6 convert_reduce_fusion.1
  217.2 7.1 %fusion.100 = f32[640,25,128]{2,0,1:T(8,128)} fusion(bf16[25,128,1024]{2,1,0:T(8,128)(2,1)S(1)} %bitcast.266, bf16[1,640,1024]{1,2,0:T(8,128)(2,1)S(1)} %get-tuple-element.57), kind=kOutput, calls=%fused_computation.180 | convolution fusion | flops 4194304000 | bytes 16056320 | tf_op jit(solution)/shard_map/rol,rkcil->okci/dot_general | solution.py:288
  224.4 17.2 %reduce-scatter.9.cloned.1.call-done.refs_0_ = f32[4,200,128]{2,1,0:T(8,128)} async-done(((f32[4,800,128]{2,1,0:T(8,128)}), f32[4,200,128]{2,1,0:T(8,128)}) %reduce-scatter.9.cloned.1.call-update) | async-done | bytes 409616 | tf_op jit(solution)/shard_map/reduce_scatter | solution.py:279
  241.7 5.9 %copy.54 = f32[1,1280,1024]{1,2,0:T(8,128)} copy(f32[1,1280,1024]{2,1,0:T(8,128)} %bitcast.260) | data formatting | bytes 10485760 | tf_op jit(solution)/shard_map/convert_element_type | solution.py:257
  247.6 2.9 convert_reduce_fusion.3
  251.9 12.4 %fusion.12 = bf16[1,1280,1024]{1,2,0:T(8,128)(2,1)} fusion(f32[1,1280,1024]{1,2,0:T(8,128)} %copy.54, bf16[640,1280]{1,0:T(8,128)(2,1)} %bitcast.277, f32[1280]{0:T(1024)S(1)} %add.218, f32[640]{0:T(1024)S(1)} %add.214, f32[640]{0:T(1024)S(1)} %mul.461, f32[1024]{0:T(1024)S(1)} %add_rsqrt_fusion, f32[1024]{0:T(1024)S(1)} %broadcast_multiply_fusion.4, ...), kind=kOutput, calls=%fused_computation.15 | convolution fusion | flops 1727528960 | bytes 12145152 | tf_op jit(solution)/shard_map/hd,rhl->rdl/dot_general | solution.py:269
  264.2 4.4 copy.55
  268.6 4.5 all-to-all-start.2
  273.2 3.1 collective-permute-start.5
  276.4 8.3 %copy.53 = bf16[5,640,640]{2,1,0:T(8,128)(2,1)} copy(bf16[5,640,640]{1,2,0:T(8,128)(2,1)} %bitcast.263) | data formatting | bytes 8192000 | tf_op jit(solution)/shard_map/transpose | solution.py:296
  293.7 16.5 %fusion.56 = (f32[640]{0:T(1024)S(1)}, f32[1024]{0:T(1024)S(1)}, f32[1024]{0:T(1024)S(1)}, f32[640]{0:T(1024)S(1)}, f32[1,640,1024]{1,2,0:T(8,128)}) fusion(f32[1024]{0:T(1024)S(1)} %add_rsqrt_fusion.1, f32[1024]{0:T(1024)S(1)} %broadcast_multiply_fusion.5, f32[640]{0:T(1024)S(1)} %add.201, f32[1024,640]{1,0:T(8,128)S(1)} %copy-done.2, f32[640]{0:T(1024)S(1)} %mul.450, ...), kind=kOutput, calls=%fused_computation.100 | convolution fusion | flops 4248695808 | bytes 15921664 | tf_op jit(solution)/shard_map/oc,rol->rcl/dot_general | solution.py:297
  310.4 3.3 fusion.55
  313.7 19.4 %multiply_reduce_fusion = (f32[1280]{0:T(1024)S(1)}, f32[1024]{0:T(1024)S(1)}, f32[1024]{0:T(1024)S(1)}, f32[1280]{0:T(1024)S(1)}, f32[1,1280,1024]{1,2,0:T(8,128)}) fusion(f32[1,1280,1024]{1,2,0:T(8,128)} %copy.54, f32[1024]{0:T(1024)S(1)} %copy-done.16, f32[1024]{0:T(1024)S(1)} %copy-done.19, f32[1280]{0:T(1024)S(1)} %copy-done.13, ...), kind=kOutput, calls=%fused_computation.21 | convolution fusion | flops 1785196032 | bytes 13471744 | tf_op jit(solution)/shard_map/dh,rhl->rdl/dot_general | solution.py:305
  333.8 5.7 %fusion.57 = f32[1280,640]{1,0:T(8,128)} fusion(bf16[1,1280,1,1,1,1,1024]{6,1,5,4,3,2,0:T(8,128)(2,1)} %copy-done.9, bf16[1,640,1024]{1,2,0:T(8,128)(2,1)S(1)} %copy-done.7), kind=kOutput, calls=%fused_computation.102 | convolution fusion | flops 1677721600 | bytes 7208960 | tf_op jit(solution)/shard_map/rdl,rhl->dh/dot_general | solution.py:304
  339.5 2.8 reshape.1459
  342.3 7.8 %shard_map.256 = f32[3,200,128]{2,1,0:T(8,128)} custom-call(f32[4,200,128]{2,1,0:T(8,128)} %reduce-scatter.9.cloned.1.call-done.refs_0_), custom_call_target="tpu_custom_call" | custom-call | bytes 819200 | tf_op jit(solution)/shard_map/pallas_call | solution.py:87
  352.0 20.1 %all_gather.34 = f32[4,200,128]{2,1,0:T(8,128)S(1)} all-gather(f32[1,200,128]{2,1,0:T(8,128)S(1)} %bitcast_add_fusion.4), channel_id=1, replica_groups=mesh['batch'=4,'seq'=2,'ch'=4] {'batch'}, dimensions={0}, use_global_device_ids=true | all-gather | bytes 512000 | tf_op jit(solution)/shard_map/all_gather | solution.py:337
  372.0 2.5 all_gather.35
  380.7 21.3 %shard_map.255 = f32[80,5,3,160]{3,2,1,0:T(4,128)} custom-call(f32[80,5,4,160]{3,2,1,0:T(4,128)} %reshape.1457.refs_0_), custom_call_target="tpu_custom_call" | custom-call | bytes 2048000 | tf_op jit(solution)/shard_map/pallas_call | solution.py:87
  402.0 2.4 reduce_sum.234
  404.7 2.6 dynamic-slice_reduce_fusion
  407.6 21.1 %all_gather.32 = f32[4,500,128]{2,1,0:T(8,128)} all-gather(f32[1,500,128]{2,1,0:T(8,128)S(1)} %add.224), channel_id=1, replica_groups=mesh['batch'=4,'seq'=2,'ch'=4] {'batch'}, dimensions={0}, use_global_device_ids=true | all-gather | bytes 1280000 | tf_op jit(solution)/shard_map/all_gather | solution.py:337
  428.8 4.9 copy.57
  433.7 7.3 %add_convert_fusion = bf16[1,1280,1024]{1,2,0:T(8,128)(2,1)S(1)} fusion(f32[1,1280,1024]{1,2,0:T(8,128)} %copy.57, f32[1,1280,1024]{1,2,0:T(8,128)} %get-tuple-element.88, f32[1,1280,1024]{1,2,0:T(8,128)} %copy.54, f32[1024]{0:T(1024)S(1)} %broadcast_multiply_fusion.6, f32[1024]{0:T(1024)S(1)} %broadcast_multiply_fusion.7, f32[1280]{0:T(1024)S(1)} %copy-done.13, ...), kind=kLoop, calls=%fused_computation.22 | loop fusion | flops 11796480 | bytes 18371584 | tf_op jit(solution)/shard_map/convert_element_type | solution.py:309
  441.1 4.8 reshape.1458
  445.9 2.6 copy.61
  448.5 3.8 all-to-all-start.3
  453.3 5.1 copy.62
  458.4 23.7 %all-to-all-done.3 = bf16[4,320,1024]{2,1,0:T(8,128)(2,1)S(1)} async-done(((bf16[4,320,1024]{2,1,0:T(8,128)(2,1)}), bf16[4,320,1024]{2,1,0:T(8,128)(2,1)S(1)}, u32[]{:S(2)}, u32[]{:S(2)}) %all-to-all-start.3) | async-done | bytes 2621472 | tf_op jit(solution)/shard_map/all_to_all | solution.py:185
  482.1 7.1 %shard_map.257 = f32[3,208,128]{2,1,0:T(8,128)} custom-call(f32[4,208,128]{2,1,0:T(8,128)} %reduce-scatter.17.cloned.1.call-done.refs_0_), custom_call_target="tpu_custom_call" | custom-call | bytes 851968 | tf_op jit(solution)/shard_map/pallas_call | solution.py:87
  491.1 15.3 %all_gather.36 = f32[4,208,128]{2,1,0:T(8,128)S(1)} all-gather(f32[1,208,128]{2,1,0:T(8,128)S(1)} %bitcast_add_fusion.3), channel_id=1, replica_groups=mesh['batch'=4,'seq'=2,'ch'=4] {'batch'}, dimensions={0}, use_global_device_ids=true | all-gather | bytes 532480 | tf_op jit(solution)/shard_map/all_gather | solution.py:337
  511.3 3.5 copy.83
  (163 shorter events, 60.9 us)
Async XLA Ops:
  7.2 52.0 %copy-start.10 = (bf16[320,640]{1,0:T(8,128)(2,1)S(1)}, bf16[320,640]{1,0:T(8,128)(2,1)}, u32[]{:S(2)}) copy-start(bf16[320,640]{1,0:T(8,128)(2,1)} %param.19) | copy-start | bytes 1228804
  7.2 109.7 %all-gather.5.cloned.1.call-start = ((), (), s32[]{:S(2)}) async-start(), calls=%async_computation.10 | async-start | bytes 2457600 | tf_op jit(solution)/shard_map/all_gather | solution.py:242
  59.9 34.5 %all-to-all-start = ((bf16[4,320,1024]{2,1,0:T(8,128)(2,1)}), bf16[4,320,1024]{2,1,0:T(8,128)(2,1)S(1)}, u32[]{:S(2)}, u32[]{:S(2)}) async-start(bf16[4,320,1024]{2,1,0:T(8,128)(2,1)} %param.15), calls=%async_computation | async-start | bytes 5242880 | tf_op jit(solution)/shard_map/all_to_all | solution.py:172
  63.6 7.1 %copy-start.14 = (f32[1920]{0:T(1024)S(1)}, f32[1920]{0:T(1024)}, u32[]{:S(2)}) copy-start(f32[1920]{0:T(1024)} %concatenate.42.refs_0_) | copy-start | bytes 23044
  63.6 7.1 %copy-start.17 = (f32[4,1920]{1,0:T(4,128)S(1)}, f32[4,1920]{1,0:T(4,128)}, u32[]{:S(2)}) copy-start(f32[4,1920]{1,0:T(4,128)} %get-tuple-element.26) | copy-start | bytes 92164
  63.6 83.1 %all-gather.7.cloned.1.call-start = ((), (), s32[]{:S(2)}) async-start(), calls=%async_computation.11 | async-start | bytes 6144000 | tf_op jit(solution)/shard_map/all_gather | solution.py:243
  64.5 66.4 %collective-permute-start = (s32[1,64]{1,0:T(1,128)S(1)}, s32[1,64]{1,0:T(1,128)S(1)}, u32[]{:S(2)}, u32[]{:S(2)}) collective-permute-start(s32[1,64]{1,0:T(1,128)S(1)} %get-tuple-element.81), channel_id=1, source_target_pairs={{4,0},{5,1},{6,2},{7,3},{12,8},{13,9},{14,10},{15,11},{20,16},{21,... | collective-permute-start | bytes 776 | tf_op jit(solution)/shard_map/ppermute | solution.py:152
  65.8 65.2 %collective-permute-start.1 = (s32[1,64]{1,0:T(1,128)S(1)}, s32[1,64]{1,0:T(1,128)S(1)}, u32[]{:S(2)}, u32[]{:S(2)}) collective-permute-start(s32[1,64]{1,0:T(1,128)S(1)} %get-tuple-element.80), channel_id=1, source_target_pairs={{0,4},{1,5},{2,6},{3,7},{8,12},{9,13},{10,14},{11,15},{16,20},{17,... | collective-permute-start | bytes 776 | tf_op jit(solution)/shard_map/ppermute | solution.py:151
  71.0 29.9 %copy-start.12 = (f32[1280]{0:T(1024)}, f32[1280]{0:T(1024)S(1)}, u32[]{:S(2)}) copy-start(f32[1280]{0:T(1024)S(1)} %mul.439) | copy-start | bytes 15364
  71.1 29.8 %copy-start.20 = (f32[1280]{0:T(1024)}, f32[1280]{0:T(1024)S(1)}, u32[]{:S(2)}) copy-start(f32[1280]{0:T(1024)S(1)} %add.198) | copy-start | bytes 15364
  94.4 64.9 %all-to-all-start.1 = ((bf16[4,320,1024]{2,1,0:T(8,128)(2,1)}), bf16[4,320,1024]{2,1,0:T(8,128)(2,1)}, u32[]{:S(2)}, u32[]{:S(2)}) async-start(bf16[4,320,1024]{2,1,0:T(8,128)(2,1)} %param.29), calls=%async_computation.1 | async-start | bytes 5242880 | tf_op jit(solution)/shard_map/all_to_all | solution.py:172
  99.0 90.2 %reduce-scatter.7.cloned.1.call-start = ((), (), s32[]{:S(2)}) async-start(), calls=%async_computation.13 | async-start | bytes 4915200 | tf_op jit(solution)/shard_map/reduce_scatter | solution.py:278
  99.5 1.4 copy-start.15
  100.3 0.7 copy-start.18
  100.9 2.3 copy-start
  116.9 4.8 copy-start.9
  121.7 14.1 %copy-start.1 = (f32[1024,640]{1,0:T(8,128)}, f32[1024,640]{1,0:T(8,128)S(1)}, u32[]{:S(2)}) copy-start(f32[1024,640]{1,0:T(8,128)S(1)} %get-tuple-element.83) | copy-start | bytes 7864324
  129.6 3.2 collective-permute-start.2
  131.1 12.7 %collective-permute-start.3 = (bf16[1,640,64]{1,2,0:T(8,128)(2,1)S(1)}, bf16[1,640,64]{1,2,0:T(8,128)(2,1)S(1)}, u32[]{:S(2)}, u32[]{:S(2)}) collective-permute-start(bf16[1,640,64]{1,2,0:T(8,128)(2,1)S(1)} %get-tuple-element.60), channel_id=1, source_target_pairs={{4,0},{5,1},{6,2},{7,3},{12,8},{13,9},{14,10},{15,11},{20,16},{21,... | collective-permute-start | bytes 245768 | tf_op jit(solution)/shard_map/ppermute | solution.py:152
  149.3 9.4 %copy-start.3 = (bf16[5,4,160,640]{3,2,1,0:T(8,128)(2,1)}, bf16[5,4,160,640]{3,2,1,0:T(8,128)(2,1)S(1)}, u32[]{:S(2)}) copy-start(bf16[5,4,160,640]{3,2,1,0:T(8,128)(2,1)S(1)} %copy.50) | copy-start | bytes 12288004
  158.7 43.1 %copy-start.4 = (f32[1024,640]{1,0:T(8,128)}, f32[1024,640]{1,0:T(8,128)S(1)}, u32[]{:S(2)}) copy-start(f32[1024,640]{1,0:T(8,128)S(1)} %get-tuple-element.85) | copy-start | bytes 7864324
  175.6 1.0 copy-start.11
  175.6 26.2 %all-gather.9.cloned.1.call-start = ((), (), s32[]{:S(2)}) async-start(), calls=%async_computation.12 | async-start | bytes 2457600 | tf_op jit(solution)/shard_map/all_gather | solution.py:244
  177.3 64.3 %reduce-scatter.9.cloned.1.call-start = ((), (), s32[]{:S(2)}) async-start(), calls=%async_computation.14 | async-start | bytes 2048000 | tf_op jit(solution)/shard_map/reduce_scatter | solution.py:279
  189.3 102.7 %reduce-scatter.11.cloned.1.call-start = ((), (), s32[]{:S(2)}) async-start(), calls=%async_computation.15 | async-start | bytes 12288000 | tf_op jit(solution)/shard_map/reduce_scatter | solution.py:278
  213.6 3.6 copy-start.6
  247.6 4.3 copy-start.5
  250.5 34.4 %collective-permute-start.4 = (bf16[1,640,64]{1,2,0:T(8,128)(2,1)S(1)}, bf16[1,640,64]{1,2,0:T(8,128)(2,1)S(1)}, u32[]{:S(2)}, u32[]{:S(2)}) collective-permute-start(bf16[1,640,64]{1,2,0:T(8,128)(2,1)S(1)} %get-tuple-element.59), channel_id=1, source_target_pairs={{4,0},{5,1},{6,2},{7,3},{12,8},{13,9},{14,10},{15,11},{20,16},{21,... | collective-permute-start | bytes 245768 | tf_op jit(solution)/shard_map/ppermute | solution.py:152
  268.6 45.1 %all-to-all-start.2 = ((bf16[4,320,1024]{2,1,0:T(8,128)(2,1)}), bf16[4,320,1024]{2,1,0:T(8,128)(2,1)}, u32[]{:S(2)}, u32[]{:S(2)}) async-start(bf16[4,320,1024]{2,1,0:T(8,128)(2,1)} %bitcast.264), calls=%async_computation.4 | async-start | bytes 5242880 | tf_op jit(solution)/shard_map/all_to_all | solution.py:185
  273.2 103.5 %reduce-scatter.13.cloned.1.call-start = ((), (), s32[]{:S(2)}) async-start(), calls=%async_computation.16 | async-start | bytes 5120000 | tf_op jit(solution)/shard_map/reduce_scatter | solution.py:279
  273.2 15.9 %collective-permute-start.5 = (bf16[1,640,64]{1,2,0:T(8,128)(2,1)S(1)}, bf16[1,640,64]{1,2,0:T(8,128)(2,1)S(1)}, u32[]{:S(2)}, u32[]{:S(2)}) collective-permute-start(bf16[1,640,64]{1,2,0:T(8,128)(2,1)S(1)} %get-tuple-element.58), channel_id=1, source_target_pairs={{0,4},{1,5},{2,6},{3,7},{8,12},{9,13},{10,14},{11,15},{16,20},{17,... | collective-permute-start | bytes 245768 | tf_op jit(solution)/shard_map/ppermute | solution.py:151
  292.0 1.7 copy-start.2
  292.0 141.7 %reduce-scatter.15.cloned.1.call-start = ((), (), s32[]{:S(2)}) async-start(), calls=%async_computation.18 | async-start | bytes 5111808 | tf_op jit(solution)/shard_map/reduce_scatter | solution.py:278
  310.4 3.3 copy-start.13
  310.4 3.3 copy-start.16
  310.4 3.3 copy-start.19
  310.4 3.3 copy-start.21
  313.7 19.6 %copy-start.7 = (bf16[1,640,1024]{1,2,0:T(8,128)(2,1)S(1)}, bf16[1,640,1024]{1,2,0:T(8,128)(2,1)}, u32[]{:S(2)}) copy-start(bf16[1,640,1024]{1,2,0:T(8,128)(2,1)} %fusion.55) | copy-start | bytes 3932164
  380.6 60.4 %all-gather.11.cloned.1.call-start = ((), (), s32[]{:S(2)}) async-start(), calls=%async_computation.17 | async-start | bytes 3096576 | tf_op jit(solution)/shard_map/all_gather | solution.py:338
  428.7 53.4 %reduce-scatter.17.cloned.1.call-start = ((), (), s32[]{:S(2)}) async-start(), calls=%async_computation.19 | async-start | bytes 2129920 | tf_op jit(solution)/shard_map/reduce_scatter | solution.py:279
  448.5 3.8 copy-start.8
  448.5 33.6 %all-to-all-start.3 = ((bf16[4,320,1024]{2,1,0:T(8,128)(2,1)}), bf16[4,320,1024]{2,1,0:T(8,128)(2,1)S(1)}, u32[]{:S(2)}, u32[]{:S(2)}) async-start(bf16[4,320,1024]{2,1,0:T(8,128)(2,1)} %bitcast.265), calls=%async_computation.7 | async-start | bytes 5242880 | tf_op jit(solution)/shard_map/all_to_all | solution.py:185
Sparse Core Ops, SparseCore 0:
  60.0 11.0 all-gather.4
  72.7 14.6 all-gather.6
  175.7 13.4 reduce-scatter.6
  190.7 11.0 all-gather.8
  204.1 37.4 reduce-scatter.8
  243.7 15.7 reduce-scatter.10
  292.1 80.1 reduce-scatter.12
  380.7 9.6 reduce-scatter.14
  428.8 9.8 all-gather.10
  441.0 38.4 reduce-scatter.16

commit v3 on v2

--- a/solution.py
+++ b/solution.py
@@ -239,9 +239,10 @@
         full.append(small_all[:, cut : cut + n].reshape(n * nch))
         cut += n
     g0, s0, b_in, g1, s1, b_cv, g2, s2, b_out = full
-    w_in = lax.all_gather(w_in, "seq", axis=1, tiled=True).reshape(dim, hid)
-    w_cv = lax.all_gather(w_cv, "seq", axis=2, tiled=True).transpose(1, 0, 2, 3).reshape(KERNEL_TAPS, hid, hid)
-    w_out = lax.all_gather(w_out, "seq", axis=1, tiled=True).reshape(hid, dim)
+    w_in, w_cv, w_out = exchange([w_in, w_cv, w_out], ("seq",), 4, gather=True)
+    w_in = w_in.transpose(1, 0, 2, 3).reshape(dim, hid)
+    w_cv = w_cv.transpose(2, 1, 0, 3, 4).reshape(KERNEL_TAPS, hid, hid)
+    w_out = w_out.transpose(1, 0, 2, 3).reshape(hid, dim)
 
     x = to_positions(inputs, nch, q_count)
     cot = to_positions(cotangent, nch, q_count)

time: 532 us -> 519 us (0.976)
  waiting for transfers between devices: 78.6 us -> 40 us
  Pallas kernels: 81.5 us -> 105 us
  local copies, waits for them, and re-layouts: 90.1 us -> 101 us
  matrix products: 98.8 us -> 91.8 us
    pallas_call x4 -> x5, Pallas kernels: 81.5 us -> 105 us  [exchange(): pl.pallas_call(functools.partial(_exchange_kernel, sizes, group, gather,...]
    all_to_all x2, waiting for transfers between devices: 22.8 us -> 0.01 us  [to_positions(): x = lax.all_to_all(x, 'ch', 0, 0, tiled=True)]
    all_gather x3 -> x0, waiting for transfers between devices: 12.5 us -> none  [the longest x1 12.5 us: local(): w_out = lax.all_gather(w_out, 'seq', axis=1, tiled=True).reshape(hid, dim)]
    transpose x1 -> x3, local copies, waits for them, and re-layouts: 2.64 us -> 9.94 us  [the longest x1 4.52 us: local(): w_cv = w_cv.transpose(2, 1, 0, 3, 4).reshape(KERNEL_TAPS, hid, hid)]
    dynamic_update_slice x4 -> x7, local copies, waits for them, and re-layouts: 3.41 us -> 9.35 us  [exchange(): placed.append(lax.dynamic_update_index_in_dim(out, own, me, axis))]
    unnamed x49 -> x77, local copies, waits for them, and re-layouts: 12.2 us -> 12.5 us
  transfers between devices with their start and end apart: 20 -> 17, of which waited for: 5 -> 2; matrix products, arithmetic and copies ran while one was open for 41% -> 43% of each run, Pallas kernels for 6% -> 19%
where the time goes in v3:
time: 519 us; the launch traced here: 509 us
  Pallas kernels  105 us (20%)
  local copies, waits for them, and re-layouts  101 us (19%)
  matrix products  91.8 us (18%)
  other arithmetic  64.1 us (12%)
  blocking collectives  61.5 us (12%)
  waiting for transfers between devices  40 us (8%)
  starting transfers between devices  30.7 us (6%)
  between operations  15.4 us (3%)
    pallas_call x5, Pallas kernels, exchange(): pl.pallas_call(functools.partial(_exchange_kernel, sizes, group, gather,...  105 us
    all_gather x3, blocking collectives, finish(): part = lax.all_gather(part, 'batch', axis=0)  56.6 us
    all_to_all x2, waiting for transfers between devices, to_channels(): x = lax.all_to_all(x, 'ch', 0, 0, tiled=True)  23.3 us
    dot_general x1, matrix products, local(): jnp.einsum('dh,rhl->rdl', w_in, grad_inner, preferred_element_type=jnp.fl...  19.5 us
    reduce_scatter x3, waiting for transfers between devices, reduce_seq_batch(): return lax.psum_scatter(g, 'batch', scatter_dimension=split_dim, tiled=True)  16.5 us
    dot_general x1, matrix products, local(): jnp.einsum('oc,rol->rcl', kernel_back, back_taps, preferred_element_type=...  16.4 us
    convert_element_type x1, other arithmetic, local(): hidden0 = gelu_exact(normed0).astype(jnp.bfloat16)  13.7 us
    unnamed x7, other arithmetic  12.8 us
  transfers between devices with their start and end apart: 17, of which 2 were waited for; matrix products, arithmetic and copies ran while one was open for 43% of the time, Pallas kernels for 19%

profile of v3, /device:TPU:0, one launch (start us, length us, event | category | flops | bytes accessed | tf_op | source)
XLA Modules:
  0.0 509.3 jit_solution(2854238294001339469)
XLA Ops:
  7.3 5.3 %all-to-all-start = ((bf16[4,320,1024]{2,1,0:T(8,128)(2,1)}), bf16[4,320,1024]{2,1,0:T(8,128)(2,1)S(1)}, u32[]{:S(2)}, u32[]{:S(2)}) async-start(bf16[4,320,1024]{2,1,0:T(8,128)(2,1)} %param.15), calls=%async_computation | async-start | bytes 5242880 | tf_op jit(solution)/shard_map/all_to_all | solution.py:172
  14.7 3.0 collective-permute-start.1
  21.2 62.1 %shard_map.254 = (f32[4,1920]{1,0:T(4,128)}, bf16[4,160,640]{2,1,0:T(8,128)(2,1)}, bf16[4,5,80,640]{3,2,1,0:T(8,128)(2,1)}, bf16[4,80,1280]{2,1,0:T(8,128)(2,1)}) custom-call(f32[1920]{0:T(1024)} %copy-done.19, bf16[160,640]{1,0:T(8,128)(2,1)} %constant_dynamic-slice_fusion.2.refs_1_, bf16[5,80,640]{2,1,0:T(8,128)(2,1)} %constant_dynamic-slice_fusion.1.refs_2_, ...), custom_call_target="tpu_custom_call" | custom-call | bytes 7434240 | tf_op jit(solution)/shard_map/pallas_call | solution.py:87
  87.6 6.8 %shard_map.255 = (bf16[2,4,160,640]{3,2,1,0:T(8,128)(2,1)}, bf16[2,4,5,80,640]{4,3,2,1,0:T(8,128)(2,1)}, bf16[2,4,80,1280]{3,2,1,0:T(8,128)(2,1)}) custom-call(bf16[4,160,640]{2,1,0:T(8,128)(2,1)} %bitcast_dynamic-update-slice_fusion.5.refs_0_, bf16[4,5,80,640]{3,2,1,0:T(8,128)(2,1)} %bitcast_dynamic-update-slice_fusion.3.refs_1_, ...), custom_call_target="tpu_custom_call" | custom-call | bytes 14745600 | tf_op jit(solution)/shard_map/pallas_call | solution.py:87
  95.4 2.7 copy.52
  98.8 3.1 bitcast_dynamic-update-slice_fusion
  101.8 4.5 copy.53
  106.6 4.6 all-to-all-start.1
  113.1 13.7 %fusion.6 = bf16[1,1280,1,1,1,1,1024]{6,1,5,4,3,2,0:T(8,128)(2,1)S(1)} fusion(f32[1,1280,1,1,1,1,1024]{6,1,5,4,3,2,0:T(8,128)S(1)} %bitcast.267, f32[1280]{0:T(1024)S(1)} %add.206, f32[1280]{0:T(1024)S(1)} %mul.439, f32[1024]{0:T(1024)S(1)} %add_rsqrt_fusion.2, f32[1024]{0:T(1024)S(1)} %broadcast_multiply_fusion.8), kind=kLoop, calls=%fused_computation.8 | loop fusion | flops 90439680 | bytes 7882752 | tf_op jit(solution)/shard_map/convert_element_type | solution.py:260
  129.9 7.3 %multiply_convert_fusion.1 = bf16[1,640,1024]{1,2,0:T(8,128)(2,1)S(1)} fusion(f32[640]{0:T(1024)S(1)} %add.214, f32[640]{0:T(1024)S(1)} %mul.450, f32[1024]{0:T(1024)S(1)} %add_rsqrt_fusion.1, f32[1024]{0:T(1024)S(1)} %broadcast_multiply_fusion.5, f32[640]{0:T(1024)S(1)} %add.210, f32[1024,640]{1,0:T(8,128)S(1)} %get-tuple-element.89), kind=kLoop, calls=%fused_computation.123 | loop fusion | flops 45875200 | bytes 3948032 | tf_op jit(solution)/shard_map/convert_element_type | solution.py:263
  141.7 7.3 %constant_dynamic-update-slice_fusion = bf16[1,3200,1024]{1,2,0:T(8,128)(2,1)S(1)} fusion(bf16[1,3200,1024]{1,2,0:T(8,128)(2,1)S(1)} %fusion.99, f32[640]{0:T(1024)S(1)} %add.214, f32[640]{0:T(1024)S(1)} %mul.450, f32[1024]{0:T(1024)S(1)} %add_rsqrt_fusion.1, f32[1024]{0:T(1024)S(1)} %broadcast_multiply_fusion.5, f32[640]{0:T(1024)S(1)} %add.210, ...), kind=kLoop, calls=%fused_computation.196 | loop fusion | flops 45875200 | bytes 3952640
  152.2 5.5 %fusion.74 = (f32[1024]{0:T(1024)S(1)}, f32[1024,640]{1,0:T(8,128)S(1)}) fusion(f32[640]{0:T(1024)S(1)} %add.219, bf16[3200,640]{1,0:T(8,128)(2,1)S(1)} %bitcast.271, bf16[1,3200,1024]{1,2,0:T(8,128)(2,1)S(1)} %fusion.97), kind=kOutput, calls=%fused_computation.142 | convolution fusion | flops 4195613696 | bytes 13277696 | tf_op jit(solution)/shard_map/co,rcl->rol/dot_general | solution.py:267
  158.3 12.3 %fusion.107 = f32[640,1280]{1,0:T(8,128)} fusion(bf16[1280,1024]{1,0:T(8,128)(2,1)} %bitcast.19, f32[640]{0:T(1024)S(1)} %add.223, f32[640]{0:T(1024)S(1)} %mul.461, f32[1024]{0:T(1024)S(1)} %add_rsqrt_fusion, f32[1024]{0:T(1024)S(1)} %broadcast_multiply_fusion.4, f32[640]{0:T(1024)S(1)} %add.219, f32[1024,640]{1,0:T(8,128)S(1)} %get-tuple-element.91), kind=kOutput, calls=%fused_computation.226 | convolution fusion | flops 1723596800 | bytes 8535552 | tf_op jit(solution)/shard_map/rhl,rdl->hd/dot_general | solution.py:275
  170.6 4.5 reshape.1454
  177.2 2.7 copy.54
  179.9 9.7 %copy.62 = bf16[1,3200,1024]{2,1,0:T(8,128)(2,1)} copy(bf16[1,3200,1024]{1,2,0:T(8,128)(2,1)} %copy-done.6) | data formatting | bytes 13107200 | tf_op jit(solution)/shard_map/concatenate | solution.py:164
  189.6 11.6 %fusion.50 = (f32[640]{0:T(1024)S(1)}, f32[1024]{0:T(1024)S(1)}, f32[1024]{0:T(1024)S(1)}, f32[640]{0:T(1024)S(1)}, f32[1,640,1024]{1,2,0:T(8,128)S(1)}) fusion(f32[1024]{0:T(1024)S(1)} %add_rsqrt_fusion, f32[1024]{0:T(1024)S(1)} %broadcast_multiply_fusion.4, f32[640]{0:T(1024)S(1)} %add.219, f32[1024,640]{1,0:T(8,128)S(1)} %get-tuple-element.91, ...), kind=kOutput, calls=%fused_computation.89 | convolution fusion | flops 1732113152 | bytes 9531904 | tf_op jit(solution)/shard_map/hd,rdl->rhl/dot_general | solution.py:283
  201.2 2.6 convert_reduce_fusion.1
  204.9 7.1 %fusion.100 = f32[640,25,128]{2,0,1:T(8,128)} fusion(bf16[25,128,1024]{2,1,0:T(8,128)(2,1)S(1)} %bitcast.274, bf16[1,640,1024]{1,2,0:T(8,128)(2,1)S(1)} %get-tuple-element.63), kind=kOutput, calls=%fused_computation.181 | convolution fusion | flops 4194304000 | bytes 16056320 | tf_op jit(solution)/shard_map/rol,rkcil->okci/dot_general | solution.py:289
  212.0 16.5 %reduce-scatter.9.cloned.1.call-done.refs_0_ = f32[4,200,128]{2,1,0:T(8,128)} async-done(((f32[4,800,128]{2,1,0:T(8,128)}), f32[4,200,128]{2,1,0:T(8,128)}) %reduce-scatter.9.cloned.1.call-update) | async-done | bytes 409616 | tf_op jit(solution)/shard_map/reduce_scatter | solution.py:280
  228.7 7.8 %copy.57 = bf16[5,640,640]{2,1,0:T(8,128)(2,1)} copy(bf16[5,640,640]{1,2,0:T(8,128)(2,1)} %bitcast.270) | data formatting | bytes 8192000 | tf_op jit(solution)/shard_map/transpose | solution.py:297
  236.5 6.6 %copy.58 = f32[1,1280,1024]{1,2,0:T(8,128)} copy(f32[1,1280,1024]{2,1,0:T(8,128)} %bitcast.268) | data formatting | bytes 10485760 | tf_op jit(solution)/shard_map/convert_element_type | solution.py:258
  243.1 2.8 convert_reduce_fusion.3
  247.3 11.4 %fusion.12 = bf16[1,1280,1024]{1,2,0:T(8,128)(2,1)} fusion(f32[1,1280,1024]{1,2,0:T(8,128)} %copy.58, bf16[640,1280]{1,0:T(8,128)(2,1)S(1)} %bitcast.285, f32[1280]{0:T(1024)S(1)} %add.227, f32[640]{0:T(1024)S(1)} %add.223, f32[640]{0:T(1024)S(1)} %mul.461, f32[1024]{0:T(1024)S(1)} %add_rsqrt_fusion, f32[1024]{0:T(1024)S(1)} %broadcast_multiply_fusion.4, ...), kind=kOutput, calls=%fused_computation.15 | convolution fusion | flops 1727528960 | bytes 12145152 | tf_op jit(solution)/shard_map/hd,rhl->rdl/dot_general | solution.py:270
  258.6 4.4 copy.59
  263.0 4.5 all-to-all-start.2
  267.6 3.0 collective-permute-start.5
  279.7 16.4 %fusion.56 = (f32[640]{0:T(1024)S(1)}, f32[1024]{0:T(1024)S(1)}, f32[1024]{0:T(1024)S(1)}, f32[640]{0:T(1024)S(1)}, f32[1,640,1024]{1,2,0:T(8,128)}) fusion(f32[1024]{0:T(1024)S(1)} %add_rsqrt_fusion.1, f32[1024]{0:T(1024)S(1)} %broadcast_multiply_fusion.5, f32[640]{0:T(1024)S(1)} %add.210, f32[1024,640]{1,0:T(8,128)S(1)} %copy-done.2, f32[640]{0:T(1024)S(1)} %mul.450, ...), kind=kOutput, calls=%fused_computation.100 | convolution fusion | flops 4248695808 | bytes 15921664 | tf_op jit(solution)/shard_map/oc,rol->rcl/dot_general | solution.py:298
  296.3 3.2 fusion.55
  299.5 19.5 %multiply_reduce_fusion = (f32[1280]{0:T(1024)S(1)}, f32[1024]{0:T(1024)S(1)}, f32[1024]{0:T(1024)S(1)}, f32[1280]{0:T(1024)S(1)}, f32[1,1280,1024]{1,2,0:T(8,128)}) fusion(f32[1,1280,1024]{1,2,0:T(8,128)} %copy.58, f32[1024]{0:T(1024)S(1)} %copy-done.21, f32[1024]{0:T(1024)S(1)} %copy-done.24, f32[1280]{0:T(1024)S(1)} %copy-done.18, ...), kind=kOutput, calls=%fused_computation.21 | convolution fusion | flops 1785196032 | bytes 13471744 | tf_op jit(solution)/shard_map/dh,rhl->rdl/dot_general | solution.py:306
  319.7 5.7 %fusion.57 = f32[1280,640]{1,0:T(8,128)} fusion(bf16[1,1280,1,1,1,1,1024]{6,1,5,4,3,2,0:T(8,128)(2,1)} %copy-done.12, bf16[1,640,1024]{1,2,0:T(8,128)(2,1)S(1)} %copy-done.8), kind=kOutput, calls=%fused_computation.102 | convolution fusion | flops 1677721600 | bytes 7208960 | tf_op jit(solution)/shard_map/rdl,rhl->dh/dot_general | solution.py:305
  325.3 2.7 reshape.1459
  328.1 8.4 %shard_map.257 = f32[3,200,128]{2,1,0:T(8,128)} custom-call(f32[4,200,128]{2,1,0:T(8,128)} %reduce-scatter.9.cloned.1.call-done.refs_0_), custom_call_target="tpu_custom_call" | custom-call | bytes 819200 | tf_op jit(solution)/shard_map/pallas_call | solution.py:87
  338.4 20.4 %all_gather.22 = f32[4,200,128]{2,1,0:T(8,128)S(1)} all-gather(f32[1,200,128]{2,1,0:T(8,128)S(1)} %bitcast_add_fusion.4), channel_id=1, replica_groups=mesh['batch'=4,'seq'=2,'ch'=4] {'batch'}, dimensions={0}, use_global_device_ids=true | all-gather | bytes 512000 | tf_op jit(solution)/shard_map/all_gather | solution.py:338
  358.8 2.5 all_gather.23
  367.5 20.9 %shard_map.256 = f32[80,5,3,160]{3,2,1,0:T(4,128)} custom-call(f32[80,5,4,160]{3,2,1,0:T(4,128)} %reshape.1457.refs_0_), custom_call_target="tpu_custom_call" | custom-call | bytes 2048000 | tf_op jit(solution)/shard_map/pallas_call | solution.py:87
  391.1 2.6 dynamic-slice_reduce_fusion
  394.0 20.7 %all_gather.20 = f32[4,500,128]{2,1,0:T(8,128)} all-gather(f32[1,500,128]{2,1,0:T(8,128)S(1)} %add.233), channel_id=1, replica_groups=mesh['batch'=4,'seq'=2,'ch'=4] {'batch'}, dimensions={0}, use_global_device_ids=true | all-gather | bytes 1280000 | tf_op jit(solution)/shard_map/all_gather | solution.py:338
  414.8 4.9 copy.61
  419.8 7.3 %add_convert_fusion = bf16[1,1280,1024]{1,2,0:T(8,128)(2,1)S(1)} fusion(f32[1,1280,1024]{1,2,0:T(8,128)} %copy.61, f32[1,1280,1024]{1,2,0:T(8,128)} %get-tuple-element.94, f32[1,1280,1024]{1,2,0:T(8,128)} %copy.58, f32[1024]{0:T(1024)S(1)} %broadcast_multiply_fusion.6, f32[1024]{0:T(1024)S(1)} %broadcast_multiply_fusion.7, f32[1280]{0:T(1024)S(1)} %copy-done.18, ...), kind=kLoop, calls=%fused_computation.22 | loop fusion | flops 11796480 | bytes 18371584 | tf_op jit(solution)/shard_map/convert_element_type | solution.py:310
  427.2 4.8 reshape.1458
  432.0 2.6 copy.65
  434.6 3.8 all-to-all-start.3
  439.4 5.1 %copy.66 = f32[640,5,160]{0,2,1:T(8,128)} copy(f32[640,5,160]{2,1,0:T(8,128)} %bitcast.269) | data formatting | bytes 4096000 | tf_op jit(solution)/shard_map/reshape | solution.py:351
  444.5 23.2 %all-to-all-done.3 = bf16[4,320,1024]{2,1,0:T(8,128)(2,1)S(1)} async-done(((bf16[4,320,1024]{2,1,0:T(8,128)(2,1)}), bf16[4,320,1024]{2,1,0:T(8,128)(2,1)S(1)}, u32[]{:S(2)}, u32[]{:S(2)}) %all-to-all-start.3) | async-done | bytes 2621472 | tf_op jit(solution)/shard_map/all_to_all | solution.py:185
  467.8 7.1 %shard_map.258 = f32[3,208,128]{2,1,0:T(8,128)} custom-call(f32[4,208,128]{2,1,0:T(8,128)} %reduce-scatter.17.cloned.1.call-done.refs_0_), custom_call_target="tpu_custom_call" | custom-call | bytes 851968 | tf_op jit(solution)/shard_map/pallas_call | solution.py:87
  476.8 15.5 %all_gather.24 = f32[4,208,128]{2,1,0:T(8,128)S(1)} all-gather(f32[1,208,128]{2,1,0:T(8,128)S(1)} %bitcast_add_fusion.3), channel_id=1, replica_groups=mesh['batch'=4,'seq'=2,'ch'=4] {'batch'}, dimensions={0}, use_global_device_ids=true | all-gather | bytes 532480 | tf_op jit(solution)/shard_map/all_gather | solution.py:338
  497.1 3.5 copy.90
  (188 shorter events, 59.4 us)
Async XLA Ops:
  7.2 10.6 %copy-start.27 = (f32[320]{0:T(512)S(1)}, f32[320]{0:T(512)}, u32[]{:S(2)}) copy-start(f32[320]{0:T(512)} %param.17) | copy-start | bytes 3844
  7.2 10.6 %copy-start.28 = (f32[320]{0:T(512)S(1)}, f32[320]{0:T(512)}, u32[]{:S(2)}) copy-start(f32[320]{0:T(512)} %param.18) | copy-start | bytes 3844
  7.2 10.6 %copy-start.30 = (f32[160]{0:T(256)S(1)}, f32[160]{0:T(256)}, u32[]{:S(2)}) copy-start(f32[160]{0:T(256)} %param.20) | copy-start | bytes 1924
  7.2 10.6 %copy-start.31 = (f32[160]{0:T(256)S(1)}, f32[160]{0:T(256)}, u32[]{:S(2)}) copy-start(f32[160]{0:T(256)} %param.21) | copy-start | bytes 1924
  7.2 10.6 %copy-start.32 = (f32[160]{0:T(256)S(1)}, f32[160]{0:T(256)}, u32[]{:S(2)}) copy-start(f32[160]{0:T(256)} %param.22) | copy-start | bytes 1924
  7.2 10.6 %copy-start.33 = (f32[160]{0:T(256)S(1)}, f32[160]{0:T(256)}, u32[]{:S(2)}) copy-start(f32[160]{0:T(256)} %param.24) | copy-start | bytes 1924
  7.2 10.6 %copy-start.34 = (f32[160]{0:T(256)S(1)}, f32[160]{0:T(256)}, u32[]{:S(2)}) copy-start(f32[160]{0:T(256)} %param.25) | copy-start | bytes 1924
  7.3 10.6 %copy-start.35 = (f32[160]{0:T(256)S(1)}, f32[160]{0:T(256)}, u32[]{:S(2)}) copy-start(f32[160]{0:T(256)} %param.26) | copy-start | bytes 1924
  7.3 10.6 %copy-start.29 = (f32[320]{0:T(512)S(1)}, f32[320]{0:T(512)}, u32[]{:S(2)}) copy-start(f32[320]{0:T(512)} %param.28) | copy-start | bytes 3844
  7.3 10.7 %copy-start.15 = (bf16[320,640]{1,0:T(8,128)(2,1)S(1)}, bf16[320,640]{1,0:T(8,128)(2,1)}, u32[]{:S(2)}) copy-start(bf16[320,640]{1,0:T(8,128)(2,1)} %param.19) | copy-start | bytes 1228804
  7.3 13.2 %copy-start.16 = (bf16[160,1280]{1,0:T(8,128)(2,1)S(1)}, bf16[160,1280]{1,0:T(8,128)(2,1)}, u32[]{:S(2)}) copy-start(bf16[160,1280]{1,0:T(8,128)(2,1)} %param.27) | copy-start | bytes 1228804
  7.3 99.3 %all-to-all-start = ((bf16[4,320,1024]{2,1,0:T(8,128)(2,1)}), bf16[4,320,1024]{2,1,0:T(8,128)(2,1)S(1)}, u32[]{:S(2)}, u32[]{:S(2)}) async-start(bf16[4,320,1024]{2,1,0:T(8,128)(2,1)} %param.15), calls=%async_computation | async-start | bytes 5242880 | tf_op jit(solution)/shard_map/all_to_all | solution.py:172
  13.4 125.9 %collective-permute-start = (s32[1,64]{1,0:T(1,128)S(1)}, s32[1,64]{1,0:T(1,128)S(1)}, u32[]{:S(2)}, u32[]{:S(2)}) collective-permute-start(s32[1,64]{1,0:T(1,128)S(1)} %get-tuple-element.87), channel_id=1, source_target_pairs={{4,0},{5,1},{6,2},{7,3},{12,8},{13,9},{14,10},{15,11},{20,16},{21,... | collective-permute-start | bytes 776 | tf_op jit(solution)/shard_map/ppermute | solution.py:152
  14.7 124.6 %collective-permute-start.1 = (s32[1,64]{1,0:T(1,128)S(1)}, s32[1,64]{1,0:T(1,128)S(1)}, u32[]{:S(2)}, u32[]{:S(2)}) collective-permute-start(s32[1,64]{1,0:T(1,128)S(1)} %get-tuple-element.86), channel_id=1, source_target_pairs={{0,4},{1,5},{2,6},{3,7},{8,12},{9,13},{10,14},{11,15},{16,20},{17,... | collective-permute-start | bytes 776 | tf_op jit(solution)/shard_map/ppermute | solution.py:151
  17.9 3.3 copy-start.19
  84.0 10.4 %copy-start.10 = (bf16[4,160,640]{2,1,0:T(8,128)(2,1)S(1)}, bf16[4,160,640]{2,1,0:T(8,128)(2,1)}, u32[]{:S(2)}) copy-start(bf16[4,160,640]{2,1,0:T(8,128)(2,1)} %bitcast_dynamic-update-slice_fusion.5.refs_0_) | copy-start | bytes 2457604
  94.4 3.7 copy-start.22
  98.4 14.7 %copy-start.17 = (f32[1280]{0:T(1024)}, f32[1280]{0:T(1024)S(1)}, u32[]{:S(2)}) copy-start(f32[1280]{0:T(1024)S(1)} %mul.439) | copy-start | bytes 15364
  98.5 14.6 %copy-start.25 = (f32[1280]{0:T(1024)}, f32[1280]{0:T(1024)S(1)}, u32[]{:S(2)}) copy-start(f32[1280]{0:T(1024)S(1)} %add.206) | copy-start | bytes 15364
  106.6 51.7 %all-to-all-start.1 = ((bf16[4,320,1024]{2,1,0:T(8,128)(2,1)}), bf16[4,320,1024]{2,1,0:T(8,128)(2,1)}, u32[]{:S(2)}, u32[]{:S(2)}) async-start(bf16[4,320,1024]{2,1,0:T(8,128)(2,1)} %param.29), calls=%async_computation.1 | async-start | bytes 5242880 | tf_op jit(solution)/shard_map/all_to_all | solution.py:172
  111.2 78.4 %reduce-scatter.7.cloned.1.call-start = ((), (), s32[]{:S(2)}) async-start(), calls=%async_computation.10 | async-start | bytes 4915200 | tf_op jit(solution)/shard_map/reduce_scatter | solution.py:279
  113.1 13.8 %copy-start = (f32[4,320,1024]{2,1,0:T(8,128)}, f32[4,320,1024]{2,1,0:T(8,128)S(1)}, u32[]{:S(2)}) copy-start(f32[4,320,1024]{2,1,0:T(8,128)S(1)} %convert_element_type.152) | copy-start | bytes 15728644
  113.1 13.8 %copy-start.13 = (bf16[4,2,160,640]{3,2,1,0:T(8,128)(2,1)S(1)}, bf16[4,2,160,640]{3,2,1,0:T(8,128)(2,1)}, u32[]{:S(2)}) copy-start(bf16[4,2,160,640]{3,2,1,0:T(8,128)(2,1)} %copy.52) | copy-start | bytes 4915204
  129.3 12.4 %copy-start.1 = (f32[1024,640]{1,0:T(8,128)}, f32[1024,640]{1,0:T(8,128)S(1)}, u32[]{:S(2)}) copy-start(f32[1024,640]{1,0:T(8,128)S(1)} %get-tuple-element.89) | copy-start | bytes 7864324
  137.2 3.7 collective-permute-start.2
  139.4 9.6 %collective-permute-start.3 = (bf16[1,640,64]{1,2,0:T(8,128)(2,1)S(1)}, bf16[1,640,64]{1,2,0:T(8,128)(2,1)S(1)}, u32[]{:S(2)}, u32[]{:S(2)}) collective-permute-start(bf16[1,640,64]{1,2,0:T(8,128)(2,1)S(1)} %get-tuple-element.66), channel_id=1, source_target_pairs={{4,0},{5,1},{6,2},{7,3},{12,8},{13,9},{14,10},{15,11},{20,16},{21,... | collective-permute-start | bytes 245768 | tf_op jit(solution)/shard_map/ppermute | solution.py:152
  149.1 3.2 copy-start.3
  149.9 7.8 %copy-start.6 = (bf16[1,3200,1024]{1,2,0:T(8,128)(2,1)}, bf16[1,3200,1024]{1,2,0:T(8,128)(2,1)S(1)}, u32[]{:S(2)}) copy-start(bf16[1,3200,1024]{1,2,0:T(8,128)(2,1)S(1)} %fusion.97) | copy-start | bytes 19660804
  157.7 31.9 %copy-start.4 = (f32[1024,640]{1,0:T(8,128)}, f32[1024,640]{1,0:T(8,128)S(1)}, u32[]{:S(2)}) copy-start(f32[1024,640]{1,0:T(8,128)S(1)} %get-tuple-element.91) | copy-start | bytes 7864324
  175.1 53.4 %reduce-scatter.9.cloned.1.call-start = ((), (), s32[]{:S(2)}) async-start(), calls=%async_computation.11 | async-start | bytes 2048000 | tf_op jit(solution)/shard_map/reduce_scatter | solution.py:280
  189.6 88.4 %reduce-scatter.11.cloned.1.call-start = ((), (), s32[]{:S(2)}) async-start(), calls=%async_computation.12 | async-start | bytes 12288000 | tf_op jit(solution)/shard_map/reduce_scatter | solution.py:279
  201.2 3.7 copy-start.7
  236.5 10.8 %copy-start.14 = (bf16[4,2,80,1280]{3,2,1,0:T(8,128)(2,1)S(1)}, bf16[4,2,80,1280]{3,2,1,0:T(8,128)(2,1)}, u32[]{:S(2)}) copy-start(bf16[4,2,80,1280]{3,2,1,0:T(8,128)(2,1)} %copy.54) | copy-start | bytes 4915204
  243.1 4.2 copy-start.5
  246.0 24.9 %collective-permute-start.4 = (bf16[1,640,64]{1,2,0:T(8,128)(2,1)S(1)}, bf16[1,640,64]{1,2,0:T(8,128)(2,1)S(1)}, u32[]{:S(2)}, u32[]{:S(2)}) collective-permute-start(bf16[1,640,64]{1,2,0:T(8,128)(2,1)S(1)} %get-tuple-element.65), channel_id=1, source_target_pairs={{4,0},{5,1},{6,2},{7,3},{12,8},{13,9},{14,10},{15,11},{20,16},{21,... | collective-permute-start | bytes 245768 | tf_op jit(solution)/shard_map/ppermute | solution.py:152
  263.0 36.5 %all-to-all-start.2 = ((bf16[4,320,1024]{2,1,0:T(8,128)(2,1)}), bf16[4,320,1024]{2,1,0:T(8,128)(2,1)}, u32[]{:S(2)}, u32[]{:S(2)}) async-start(bf16[4,320,1024]{2,1,0:T(8,128)(2,1)} %bitcast.272), calls=%async_computation.4 | async-start | bytes 5242880 | tf_op jit(solution)/shard_map/all_to_all | solution.py:185
  267.6 95.9 %reduce-scatter.13.cloned.1.call-start = ((), (), s32[]{:S(2)}) async-start(), calls=%async_computation.13 | async-start | bytes 5120000 | tf_op jit(solution)/shard_map/reduce_scatter | solution.py:280
  267.6 7.5 %collective-permute-start.5 = (bf16[1,640,64]{1,2,0:T(8,128)(2,1)S(1)}, bf16[1,640,64]{1,2,0:T(8,128)(2,1)S(1)}, u32[]{:S(2)}, u32[]{:S(2)}) collective-permute-start(bf16[1,640,64]{1,2,0:T(8,128)(2,1)S(1)} %get-tuple-element.64), channel_id=1, source_target_pairs={{0,4},{1,5},{2,6},{3,7},{8,12},{9,13},{10,14},{11,15},{16,20},{17,... | collective-permute-start | bytes 245768 | tf_op jit(solution)/shard_map/ppermute | solution.py:151
  278.0 141.8 %reduce-scatter.15.cloned.1.call-start = ((), (), s32[]{:S(2)}) async-start(), calls=%async_computation.15 | async-start | bytes 5111808 | tf_op jit(solution)/shard_map/reduce_scatter | solution.py:279
  296.2 3.3 copy-start.18
  296.2 3.3 copy-start.21
  296.2 3.3 copy-start.24
  296.3 3.3 copy-start.26
  299.5 19.7 %copy-start.8 = (bf16[1,640,1024]{1,2,0:T(8,128)(2,1)S(1)}, bf16[1,640,1024]{1,2,0:T(8,128)(2,1)}, u32[]{:S(2)}) copy-start(bf16[1,640,1024]{1,2,0:T(8,128)(2,1)} %fusion.55) | copy-start | bytes 3932164
  367.4 59.8 %all-gather.2.cloned.1.call-start = ((), (), s32[]{:S(2)}) async-start(), calls=%async_computation.14 | async-start | bytes 3096576 | tf_op jit(solution)/shard_map/all_gather | solution.py:339
  414.8 53.0 %reduce-scatter.17.cloned.1.call-start = ((), (), s32[]{:S(2)}) async-start(), calls=%async_computation.16 | async-start | bytes 2129920 | tf_op jit(solution)/shard_map/reduce_scatter | solution.py:280
  434.6 3.8 copy-start.11
  434.6 33.2 %all-to-all-start.3 = ((bf16[4,320,1024]{2,1,0:T(8,128)(2,1)}), bf16[4,320,1024]{2,1,0:T(8,128)(2,1)S(1)}, u32[]{:S(2)}, u32[]{:S(2)}) async-start(bf16[4,320,1024]{2,1,0:T(8,128)(2,1)} %bitcast.273), calls=%async_computation.7 | async-start | bytes 5242880 | tf_op jit(solution)/shard_map/all_to_all | solution.py:185
  (5 other events, 7.4 us)
Sparse Core Ops, SparseCore 0:
  175.2 13.3 reduce-scatter.6
  191.0 37.4 reduce-scatter.8
  230.9 15.6 reduce-scatter.10
  278.1 81.2 reduce-scatter.12
  367.5 8.7 reduce-scatter.14
  414.9 10.0 all-gather.1
  427.4 38.4 reduce-scatter.16
